TPU v7x, 32 devices: a whole 2x2x4 slice. The times are simulated.
32 devices in a mesh: dx: 4 (over y, core), dy: 4 (over z), band: 2 (over x).
Axes of the slice: x: 2, y: 2, z: 4, core: 2. Of those that a mesh axis runs over, the one named last changes fastest.
Arguments:
- states: float32 [24, 32, 8, 512], P('dx', 'dy', None, 'band'), may hold values from -6 to 6
- potential: float32 [24, 32, 8], P('dx', 'dy'), may hold values from -1 to 1
Outputs:
- orthonormal: float32 [24, 32, 8, 512], P('dx', 'dy', None, 'band')
All inputs are finite; a program needn't handle non-finite values.
Results may differ from a plain program's by a relative error of at most 0.000073.
Values sent between devices are 32-bit elements; how exact they have to be, the bound alone decides.
No kernel may reach another device: no remote copies, remote signals or barrier semaphores. Data moves between devices by JAX's collectives and lax.ppermute only.
A program may use at most 64 MiB of HBM per device.

v0:
```python
import jax
import jax.numpy as jnp
from jax import lax
from jax.sharding import PartitionSpec as P

DEGREE = 3


coeffs = (
    -5369.0 / 1800.0,
    12.0 / 7.0,
    -15.0 / 56.0,
    10.0 / 189.0,
    -1.0 / 112.0,
    2.0 / 1925.0,
    -1.0 / 16632.0,
)
half_width = 5.0
centre_value = 7.0


def with_halo(cells, sides, width):
    for axis, dim in sides:
        count = lax.axis_size(axis)
        head = lax.slice_in_dim(cells, 0, width, axis=dim)
        tail = lax.slice_in_dim(cells, cells.shape[dim] - width, cells.shape[dim], axis=dim)
        cells = jnp.concatenate(
            [
                lax.ppermute(tail, axis, [(i, (i + 1) % count) for i in range(count)]),
                cells,
                lax.ppermute(head, axis, [((i + 1) % count, i) for i in range(count)]),
            ],
            axis=dim,
        )
    return cells


def apply_ham(field, potential):
    padded = with_halo(field, (("dx", 0), ("dy", 1)), 6)
    size_x = field.shape[0]
    size_y = field.shape[1]
    lap = 3.0 * coeffs[0] * field
    for shift in range(1, 7):
        near = (
            padded[6 + shift : 6 + shift + size_x, 6 : 6 + size_y]
            + padded[6 - shift : 6 - shift + size_x, 6 : 6 + size_y]
        )
        near = (
            near
            + padded[6 : 6 + size_x, 6 + shift : 6 + shift + size_y]
            + padded[6 : 6 + size_x, 6 - shift : 6 - shift + size_y]
        )
        near = near + jnp.roll(field, shift, 2) + jnp.roll(field, -shift, 2)
        lap = lap + coeffs[shift] * near
    return -0.5 * lap + potential[..., None] * field


def shards(states, potential):
    prev = states
    cur = (apply_ham(states, potential) - centre_value * states) / half_width
    for step in range(1, DEGREE):
        nxt = 2.0 * (apply_ham(cur, potential) - centre_value * cur) / half_width - prev
        prev, cur = (cur, nxt)
    block = cur.shape[3]
    cells = cur.shape[0] * cur.shape[1] * cur.shape[2]
    local = cur.reshape(cells, block)
    gathered = lax.all_gather(local, "band", axis=1, tiled=True)
    total = cells * lax.axis_size("dx") * lax.axis_size("dy")
    partial_gram = (
        jnp.dot(
            gathered.T,
            gathered,
            precision=lax.Precision.HIGHEST,
            preferred_element_type=jnp.float32,
        )
        / total
    )
    correlation = lax.psum(partial_gram, ("dx", "dy"))
    factor = jnp.linalg.cholesky(correlation)
    eye = jnp.eye(correlation.shape[0], dtype=jnp.float32)
    inverse = jax.scipy.linalg.solve_triangular(factor, eye, lower=True)
    my_rows = lax.dynamic_slice_in_dim(inverse, lax.axis_index("band") * block, block, 0)
    result = jnp.dot(
        gathered, my_rows.T, precision=lax.Precision.HIGHEST, preferred_element_type=jnp.float32
    )
    return result.reshape(cur.shape)


def solution(mesh):
    return jax.shard_map(
        shards,
        mesh=mesh,
        in_specs=(P("dx", "dy", None, "band"), P("dx", "dy", None)),
        out_specs=P("dx", "dy", None, "band"),
        check_vma=False,
    )
```

profile of v0, /device:TPU:0, one launch (start us, length us, event | category | flops | bytes accessed | tf_op | source)
XLA Modules:
  0.0 442.7 jit_solution(4787194779673460491)
XLA Ops:
  7.0 1.9 collective-permute-start
  13.8 2.6 collective-permute-done.1
  16.6 2.2 collective-permute-done
  19.1 3.7 collective-permute-start.2
  23.0 19.9 %collective-permute-done.2 = f32[18,6,8,256]{3,2,1,0:T(8,128)S(1)} collective-permute-done((f32[18,6,8,256]{3,2,1,0:T(8,128)S(1)}, f32[18,6,8,256]{3,2,1,0:T(8,128)S(1)}, u32[]{:S(2)}, u32[]{:S(2)}) %collective-permute-start.2) | collective-permute-done | bytes 884768 | tf_op jit(solution)/shard_map/ppermute | solution.py:31
  42.8 19.5 %collective-permute-done.3 = f32[18,6,8,256]{3,2,1,0:T(8,128)S(1)} collective-permute-done((f32[18,6,8,256]{3,2,1,0:T(8,128)S(1)}, f32[18,6,8,256]{3,2,1,0:T(8,128)S(1)}, u32[]{:S(2)}, u32[]{:S(2)}) %collective-permute-start.3) | collective-permute-done | bytes 884768 | tf_op jit(solution)/shard_map/ppermute | solution.py:29
  62.3 1.9 broadcast_multiply_fusion
  65.2 9.0 %collective-permute-done.4 = f32[6,8,8,256]{3,2,1,0:T(8,128)S(1)} collective-permute-done((f32[6,8,8,256]{3,2,1,0:T(8,128)S(1)}, f32[6,8,8,256]{3,2,1,0:T(8,128)S(1)}, u32[]{:S(2)}, u32[]{:S(2)}) %collective-permute-start.4) | collective-permute-done | bytes 393248 | tf_op jit(solution)/shard_map/ppermute | solution.py:31
  78.5 19.5 %collective-permute-done.6 = f32[18,6,8,256]{3,2,1,0:T(8,128)S(1)} collective-permute-done((f32[18,6,8,256]{3,2,1,0:T(8,128)S(1)}, f32[18,6,8,256]{3,2,1,0:T(8,128)S(1)}, u32[]{:S(2)}, u32[]{:S(2)}) %collective-permute-start.6) | collective-permute-done | bytes 884768 | tf_op jit(solution)/shard_map/ppermute | solution.py:31
  98.0 18.8 %collective-permute-done.7 = f32[18,6,8,256]{3,2,1,0:T(8,128)S(1)} collective-permute-done((f32[18,6,8,256]{3,2,1,0:T(8,128)S(1)}, f32[18,6,8,256]{3,2,1,0:T(8,128)S(1)}, u32[]{:S(2)}, u32[]{:S(2)}) %collective-permute-start.7) | collective-permute-done | bytes 884768 | tf_op jit(solution)/shard_map/ppermute | solution.py:29
  117.3 1.9 fusion.29
  120.0 8.4 %collective-permute-done.8 = f32[6,8,8,256]{3,2,1,0:T(8,128)S(1)} collective-permute-done((f32[6,8,8,256]{3,2,1,0:T(8,128)S(1)}, f32[6,8,8,256]{3,2,1,0:T(8,128)S(1)}, u32[]{:S(2)}, u32[]{:S(2)}) %collective-permute-start.8) | collective-permute-done | bytes 393248 | tf_op jit(solution)/shard_map/ppermute | solution.py:31
  130.4 2.6 collective-permute-start.10
  133.3 19.8 %collective-permute-done.10 = f32[18,6,8,256]{3,2,1,0:T(8,128)S(1)} collective-permute-done((f32[18,6,8,256]{3,2,1,0:T(8,128)S(1)}, f32[18,6,8,256]{3,2,1,0:T(8,128)S(1)}, u32[]{:S(2)}, u32[]{:S(2)}) %collective-permute-start.10) | collective-permute-done | bytes 884768 | tf_op jit(solution)/shard_map/ppermute | solution.py:31
  153.1 20.1 %collective-permute-done.11 = f32[18,6,8,256]{3,2,1,0:T(8,128)S(1)} collective-permute-done((f32[18,6,8,256]{3,2,1,0:T(8,128)S(1)}, f32[18,6,8,256]{3,2,1,0:T(8,128)S(1)}, u32[]{:S(2)}, u32[]{:S(2)}) %collective-permute-start.11) | collective-permute-done | bytes 884768 | tf_op jit(solution)/shard_map/ppermute | solution.py:29
  173.7 1.9 fusion.38
  175.6 10.8 %all_gather.3 = f32[384,512]{1,0:T(8,128)S(1)} all-gather(f32[384,256]{1,0:T(8,128)S(1)} %bitcast.53), channel_id=1, replica_groups=mesh['dx'=4,'dy'=4,'band'=2] {'band'}, dimensions={1}, use_global_device_ids=true | all-gather | bytes 1179648 | tf_op jit(solution)/shard_map/all_gather | solution.py:67
  186.4 2.9 convolution_multiply_fusion
  190.5 92.2 %all-reduce.3.cloned.1.call-done = f32[512,512]{0,1:T(8,128)} async-done(((f32[512,512]{0,1:T(8,128)}), f32[512,512]{0,1:T(8,128)}) %all-reduce.3.cloned.1.call-update) | async-done | bytes 1048592 | tf_op jit(solution)/shard_map/psum | solution.py:78
  285.6 11.7 %cholesky.104 = f32[128,128]{1,0:T(8,128)S(1)} custom-call(f32[128,128]{1,0:T(8,128)S(1)} %cholesky.266), custom_call_target="Cholesky" | custom-call | tf_op jit(solution)/shard_map/jit(cholesky)/cholesky | solution.py:79
  297.5 9.8 %custom-call.31 = f32[1,128,128]{1,2,0:T(8,128)S(1)} custom-call(f32[1,128,128]{2,1,0:T(8,128)S(1)} %get-tuple-element.93), custom_call_target="InvertDiagBlocksLowerTriangular" | custom-call | tf_op jit(solution)/shard_map/jit(cholesky)/cholesky | solution.py:79
  309.8 11.9 %cholesky.217 = f32[128,128]{1,0:T(8,128)S(1)} custom-call(f32[128,128]{1,0:T(8,128)S(1)} %cholesky.270), custom_call_target="Cholesky" | custom-call | tf_op jit(solution)/shard_map/jit(cholesky)/cholesky | solution.py:79
  321.7 9.8 %custom-call.32 = f32[1,128,128]{1,2,0:T(8,128)S(1)} custom-call(f32[1,128,128]{2,1,0:T(8,128)S(1)} %get-tuple-element.90), custom_call_target="InvertDiagBlocksLowerTriangular" | custom-call | tf_op jit(solution)/shard_map/jit(cholesky)/cholesky | solution.py:79
  333.1 11.7 %cholesky.238 = f32[128,128]{1,0:T(8,128)S(1)} custom-call(f32[128,128]{1,0:T(8,128)S(1)} %cholesky.275), custom_call_target="Cholesky" | custom-call | tf_op jit(solution)/shard_map/jit(cholesky)/cholesky | solution.py:79
  345.5 9.8 %custom-call.33 = f32[1,128,128]{1,2,0:T(8,128)S(1)} custom-call(f32[1,128,128]{2,1,0:T(8,128)S(1)} %get-tuple-element.87), custom_call_target="InvertDiagBlocksLowerTriangular" | custom-call | tf_op jit(solution)/shard_map/jit(cholesky)/cholesky | solution.py:79
  356.8 11.9 %cholesky.255 = f32[128,128]{1,0:T(8,128)S(1)} custom-call(f32[128,128]{1,0:T(8,128)S(1)} %convolution_subtract_fusion.5), custom_call_target="Cholesky" | custom-call | tf_op jit(solution)/shard_map/jit(cholesky)/cholesky | solution.py:79
  373.8 14.1 %while.1 = (s32[]{:T(128)}, f32[512,512]{1,0:T(8,128)}, s32[4,2]{0,1:T(2,128)S(1)}, f32[4,128,128]{2,1,0:T(8,128)}, s32[]{:T(128)}) while((s32[]{:T(128)}, f32[512,512]{1,0:T(8,128)}, s32[4,2]{0,1:T(2,128)S(1)}, f32[4,128,128]{2,1,0:T(8,128)}, s32[]{:T(128)}) %tuple.58), condition=%wide.while_cond, body=%wide.while_body.sunk | while | flops 2 | bytes 132705 | solution.py:81
  374.4 2.9 bitcast_dynamic-update-slice_fusion.2
  378.0 2.9 bitcast_dynamic-update-slice_fusion.2
  381.5 2.9 bitcast_dynamic-update-slice_fusion.2
  385.0 2.8 bitcast_dynamic-update-slice_fusion.2
  387.8 40.1 %custom-call.34 = f32[4,128,128]{1,2,0:T(8,128)S(1)} custom-call(f32[4,128,128]{2,1,0:T(8,128)} %get-tuple-element.12), custom_call_target="InvertDiagBlocksLowerTriangular" | custom-call | tf_op jit(solution)/shard_map/jit(_solve_triangular)/triangular_solve | solution.py:81
  (96 shorter events, 38.1 us)
Async XLA Ops:
  6.5 9.9 %copy-start = (f32[6,8,8,256]{3,2,1,0:T(8,128)S(1)}, f32[6,8,8,256]{3,2,1,0:T(8,128)}, u32[]{:S(2)}) copy-start(f32[6,8,8,256]{3,2,1,0:T(8,128)} %param.2) | copy-start | bytes 1179652
  6.5 276.2 %all-reduce.3.cloned.1.call-start = ((), (), s32[]{:S(2)}) async-start(), calls=%async_computation | async-start | bytes 2097152 | tf_op jit(solution)/shard_map/psum | solution.py:78
  6.5 9.9 %collective-permute-start.1 = (f32[6,8,8,256]{3,2,1,0:T(8,128)}, f32[6,8,8,256]{3,2,1,0:T(8,128)S(1)}, u32[]{:S(2)}, u32[]{:S(2)}) collective-permute-start(f32[6,8,8,256]{3,2,1,0:T(8,128)} %param.2), channel_id=1, source_target_pairs={{0,8},{8,16},{16,24},{24,0},{1,9},{9,17},{17,25},{25,1},{2,10},{10... | collective-permute-start | bytes 1179656 | tf_op jit(solution)/shard_map/ppermute | solution.py:29
  7.0 11.8 %collective-permute-start = (f32[6,8,8,256]{3,2,1,0:T(8,128)}, f32[6,8,8,256]{3,2,1,0:T(8,128)S(1)}, u32[]{:S(2)}, u32[]{:S(2)}) collective-permute-start(f32[6,8,8,256]{3,2,1,0:T(8,128)} %param.2), channel_id=1, source_target_pairs={{8,0},{16,8},{24,16},{0,24},{9,1},{17,9},{25,17},{1,25},{10,2},{18... | collective-permute-start | bytes 1179656 | tf_op jit(solution)/shard_map/ppermute | solution.py:31
  18.9 3.9 copy-start.4
  19.1 23.7 %collective-permute-start.2 = (f32[18,6,8,256]{3,2,1,0:T(8,128)S(1)}, f32[18,6,8,256]{3,2,1,0:T(8,128)S(1)}, u32[]{:S(2)}, u32[]{:S(2)}) collective-permute-start(f32[18,6,8,256]{3,2,1,0:T(8,128)S(1)} %get-tuple-element.33), channel_id=1, source_target_pairs={{2,0},{4,2},{6,4},{0,6},{3,1},{5,3},{7,5},{1,7},{10,8},{12,10},{14... | collective-permute-start | bytes 2654216 | tf_op jit(solution)/shard_map/ppermute | solution.py:31
  22.7 39.6 %collective-permute-start.3 = (f32[18,6,8,256]{3,2,1,0:T(8,128)S(1)}, f32[18,6,8,256]{3,2,1,0:T(8,128)S(1)}, u32[]{:S(2)}, u32[]{:S(2)}) collective-permute-start(f32[18,6,8,256]{3,2,1,0:T(8,128)S(1)} %get-tuple-element.34), channel_id=1, source_target_pairs={{0,2},{2,4},{4,6},{6,0},{1,3},{3,5},{5,7},{7,1},{8,10},{10,12},{12... | collective-permute-start | bytes 2654216 | tf_op jit(solution)/shard_map/ppermute | solution.py:29
  64.3 9.9 %collective-permute-start.4 = (f32[6,8,8,256]{3,2,1,0:T(8,128)S(1)}, f32[6,8,8,256]{3,2,1,0:T(8,128)S(1)}, u32[]{:S(2)}, u32[]{:S(2)}) collective-permute-start(f32[6,8,8,256]{3,2,1,0:T(8,128)S(1)} %get-tuple-element.21), channel_id=1, source_target_pairs={{8,0},{16,8},{24,16},{0,24},{9,1},{17,9},{25,17},{1,25},{10,2},{18... | collective-permute-start | bytes 1179656 | tf_op jit(solution)/shard_map/ppermute | solution.py:31
  65.0 10.8 %collective-permute-start.5 = (f32[6,8,8,256]{3,2,1,0:T(8,128)S(1)}, f32[6,8,8,256]{3,2,1,0:T(8,128)S(1)}, u32[]{:S(2)}, u32[]{:S(2)}) collective-permute-start(f32[6,8,8,256]{3,2,1,0:T(8,128)S(1)} %get-tuple-element.21), channel_id=1, source_target_pairs={{0,8},{8,16},{16,24},{24,0},{1,9},{9,17},{17,25},{25,1},{2,10},{10... | collective-permute-start | bytes 1179656 | tf_op jit(solution)/shard_map/ppermute | solution.py:29
  76.1 21.8 %collective-permute-start.6 = (f32[18,6,8,256]{3,2,1,0:T(8,128)S(1)}, f32[18,6,8,256]{3,2,1,0:T(8,128)S(1)}, u32[]{:S(2)}, u32[]{:S(2)}) collective-permute-start(f32[18,6,8,256]{3,2,1,0:T(8,128)S(1)} %get-tuple-element.31), channel_id=1, source_target_pairs={{2,0},{4,2},{6,4},{0,6},{3,1},{5,3},{7,5},{1,7},{10,8},{12,10},{14... | collective-permute-start | bytes 2654216 | tf_op jit(solution)/shard_map/ppermute | solution.py:31
  77.9 38.8 %collective-permute-start.7 = (f32[18,6,8,256]{3,2,1,0:T(8,128)S(1)}, f32[18,6,8,256]{3,2,1,0:T(8,128)S(1)}, u32[]{:S(2)}, u32[]{:S(2)}) collective-permute-start(f32[18,6,8,256]{3,2,1,0:T(8,128)S(1)} %get-tuple-element.32), channel_id=1, source_target_pairs={{0,2},{2,4},{4,6},{6,0},{1,3},{3,5},{5,7},{7,1},{8,10},{10,12},{12... | collective-permute-start | bytes 2654216 | tf_op jit(solution)/shard_map/ppermute | solution.py:29
  119.2 9.2 %collective-permute-start.8 = (f32[6,8,8,256]{3,2,1,0:T(8,128)S(1)}, f32[6,8,8,256]{3,2,1,0:T(8,128)S(1)}, u32[]{:S(2)}, u32[]{:S(2)}) collective-permute-start(f32[6,8,8,256]{3,2,1,0:T(8,128)S(1)} %fusion.29), channel_id=1, source_target_pairs={{8,0},{16,8},{24,16},{0,24},{9,1},{17,9},{25,17},{1,25},{10,2},{18... | collective-permute-start | bytes 1179656 | tf_op jit(solution)/shard_map/ppermute | solution.py:31
  119.2 10.8 %collective-permute-start.9 = (f32[6,8,8,256]{3,2,1,0:T(8,128)S(1)}, f32[6,8,8,256]{3,2,1,0:T(8,128)S(1)}, u32[]{:S(2)}, u32[]{:S(2)}) collective-permute-start(f32[6,8,8,256]{3,2,1,0:T(8,128)S(1)} %fusion.29), channel_id=1, source_target_pairs={{0,8},{8,16},{16,24},{24,0},{1,9},{9,17},{17,25},{25,1},{2,10},{10... | collective-permute-start | bytes 1179656 | tf_op jit(solution)/shard_map/ppermute | solution.py:29
  130.4 22.7 %collective-permute-start.10 = (f32[18,6,8,256]{3,2,1,0:T(8,128)S(1)}, f32[18,6,8,256]{3,2,1,0:T(8,128)S(1)}, u32[]{:S(2)}, u32[]{:S(2)}) collective-permute-start(f32[18,6,8,256]{3,2,1,0:T(8,128)S(1)} %get-tuple-element.27), channel_id=1, source_target_pairs={{2,0},{4,2},{6,4},{0,6},{3,1},{5,3},{7,5},{1,7},{10,8},{12,10},{14... | collective-permute-start | bytes 2654216 | tf_op jit(solution)/shard_map/ppermute | solution.py:31
  133.0 40.2 %collective-permute-start.11 = (f32[18,6,8,256]{3,2,1,0:T(8,128)S(1)}, f32[18,6,8,256]{3,2,1,0:T(8,128)S(1)}, u32[]{:S(2)}, u32[]{:S(2)}) collective-permute-start(f32[18,6,8,256]{3,2,1,0:T(8,128)S(1)} %get-tuple-element.28), channel_id=1, source_target_pairs={{0,2},{2,4},{4,6},{6,0},{1,3},{3,5},{5,7},{7,1},{8,10},{10,12},{12... | collective-permute-start | bytes 2654216 | tf_op jit(solution)/shard_map/ppermute | solution.py:29
  282.7 1.7 copy-start.1
  284.6 1.0 copy-start.3
  344.8 83.5 %copy-start.2 = (f32[512,512]{1,0:T(8,128)S(1)}, f32[512,512]{1,0:T(8,128)}, u32[]{:S(2)}) copy-start(f32[512,512]{1,0:T(8,128)} %fusion.157) | copy-start | bytes 3145732
Sparse Core Ops, SparseCore 0:
  189.4 93.2 all-reduce.2
where the time goes:
time: 449 us; the launch traced here: 443 us
  waiting for transfers between devices  235 us (52%)
  other arithmetic  128 us (29%)
  local copies, waits for them, and re-layouts  23.5 us (5%)
  between operations  16.8 us (4%)
  matrix products  15.7 us (3%)
  starting transfers between devices  12 us (3%)
  blocking collectives  10.8 us (2%)
    psum x1, waiting for transfers between devices, shards(): correlation = lax.psum(partial_gram, ('dx', 'dy'))  92.2 us
    another operation x14, other arithmetic, shards(): factor = jnp.linalg.cholesky(correlation)  78.9 us
    ppermute x6, waiting for transfers between devices, with_halo(): lax.ppermute(head, axis, [((i + 1) % count, i) for i in range(count)])  78.7 us
    ppermute x6, waiting for transfers between devices, with_halo(): lax.ppermute(tail, axis, [(i, (i + 1) % count) for i in range(count)])  64.4 us
    another operation x3, other arithmetic, shards(): inverse = jax.scipy.linalg.solve_triangular(factor, eye, lower=True)  41.2 us
    another operation x12, local copies, waits for them, and re-layouts  14.1 us
    all_gather x1, blocking collectives, shards(): gathered = lax.all_gather(local, 'band', axis=1, tiled=True)  10.8 us
    ppermute x6, starting transfers between devices, with_halo(): lax.ppermute(head, axis, [((i + 1) % count, i) for i in range(count)])  10.8 us
  transfers between devices with their start and end apart: 13, of which 13 were waited for; matrix products, arithmetic and copies ran while one was open for 2% of the time, Pallas kernels for 0%

commit v1 on v0

v1 whole, which is shorter than its diff:
```python
import functools

import jax
import jax.numpy as jnp
from jax import lax
from jax.experimental import pallas as pl
from jax.experimental.pallas import tpu as pltpu
from jax.sharding import PartitionSpec as P

DEGREE = 3
LANES = 128
SUBLANES = 8
PANEL = 32

coeffs = (
    -5369.0 / 1800.0,
    12.0 / 7.0,
    -15.0 / 56.0,
    10.0 / 189.0,
    -1.0 / 112.0,
    2.0 / 1925.0,
    -1.0 / 16632.0,
)
WIDTH = len(coeffs) - 1
half_width = 5.0
centre_value = 7.0
VMEM = pl.BlockSpec(memory_space=pltpu.VMEM)
HIGHEST = lax.Precision.HIGHEST


def dot(a, b, dims):
    return lax.dot_general(a, b, (dims, ((), ())), precision=HIGHEST, preferred_element_type=jnp.float32)


def swap_groups(arrays, group):
    count = len(arrays)
    lane = lax.broadcasted_iota(jnp.int32, arrays[0].shape, 1)
    bit = 1
    while bit < count:
        upper = (lane // (group * bit)) % 2 == 1
        out = list(arrays)
        for i in range(count):
            if i & bit == 0:
                low, high = arrays[i], arrays[i | bit]
                out[i] = jnp.where(upper, pltpu.roll(high, group * bit, 1), low)
                out[i | bit] = jnp.where(upper, high, pltpu.roll(low, LANES - group * bit, 1))
        arrays = out
        bit *= 2
    return arrays


def pack_kernel(nz, states_ref, potential_ref, out_ref):
    columns = states_ref.shape[0] // nz
    arrays = [states_ref[pl.ds(z, columns, stride=nz), :] for z in range(nz)]
    for g, value in enumerate(swap_groups(arrays, LANES // nz)):
        out_ref[g, :columns, :] = value
    row = lax.broadcasted_iota(jnp.int32, (nz, LANES), 0)
    lane = lax.broadcasted_iota(jnp.int32, (nz, LANES), 1)
    packed = jnp.zeros((potential_ref.shape[1], LANES), jnp.float32)
    for x in range(potential_ref.shape[0]):
        spread = jnp.where(lane == row + nz * x, 1.0, 0.0)
        packed = packed + dot(potential_ref[x], spread, ((1,), (0,)))
    for g in range(nz):
        out_ref[g, columns:, :] = packed


def filter_kernel(nz, domains_y, size_x, size_y, in_ref, out_ref, field, older, potential):
    domains = in_ref.shape[0]
    total_x = size_x * (domains // domains_y)
    total_y = size_y * domains_y
    columns = size_x * size_y
    group = LANES // nz

    def place(i, x):
        return size_x * (i // domains_y) + x, size_y * (i % domains_y)

    packed = in_ref[:, columns:, :].reshape(domains * size_y, LANES)
    source = lax.broadcasted_iota(jnp.int32, (LANES, LANES), 0)
    target = lax.broadcasted_iota(jnp.int32, (LANES, LANES), 1)
    for x in range(size_x):
        spread = jnp.where(source == nz * x + target // group, 1.0, 0.0)
        values = dot(packed, spread, ((1,), (0,)))
        for i in range(domains):
            at_x, at_y = place(i, x)
            potential[at_x, at_y : at_y + size_y, :] = values[size_y * i : size_y * (i + 1)] - centre_value
            field[WIDTH + at_x, at_y : at_y + size_y, :] = in_ref[i, size_y * x : size_y * (x + 1), :]

    weights = [0.0] * nz
    for k in range(1, WIDTH + 1):
        weights[k % nz] += coeffs[k]
        weights[-k % nz] += coeffs[k]

    for step in range(DEGREE):
        for k in range(WIDTH):
            field[k] = field[total_x + k]
            field[WIDTH + total_x + k] = field[WIDTH + k]
        scale = 1.0 / half_width if step == 0 else 2.0 / half_width

        def body(x, carry, step=step, scale=scale):
            value = field[WIDTH + x]
            lap = (3.0 * coeffs[0] + weights[0]) * value
            for k in range(1, WIDTH + 1):
                near = field[WIDTH + x + k] + field[WIDTH + x - k]
                near = near + pltpu.roll(value, k, 0) + pltpu.roll(value, total_y - k, 0)
                lap = lap + coeffs[k] * near
            for k in range(1, nz):
                lap = lap + weights[k] * pltpu.roll(value, group * k, 1)
            result = (potential[x] * value - 0.5 * lap) * scale
            if step > 0:
                result = result - older[(step - 1) % 2, x]
            older[step % 2, x] = value if step + 1 < DEGREE else result
            spare[x] = result
            return carry

        spare = older.at[2]
        lax.fori_loop(0, total_x, body, 0, unroll=2)
        if step + 1 < DEGREE:
            field[WIDTH : WIDTH + total_x] = spare[...]

    for i in range(domains):
        for x in range(size_x):
            at_x, at_y = place(i, x)
            out_ref[i, size_y * x : size_y * (x + 1), :] = older[2, at_x, at_y : at_y + size_y, :]


def unpack_kernel(nz, in_ref, out_ref):
    columns = in_ref.shape[1]
    arrays = [in_ref[g] for g in range(nz)]
    for z, value in enumerate(swap_groups(arrays, LANES // nz)):
        out_ref[pl.ds(z, columns, stride=nz), :] = value


def gram_kernel(band_ref, own_ref, other_ref, out_ref):
    own = own_ref[...]
    half = own.shape[1] // 2
    rows = ((0,), (0,))
    diagonal = dot(own, own, rows)
    out_ref[0:half] = diagonal[:half, :half]
    out_ref[half : 2 * half] = diagonal[:half, half:]
    out_ref[2 * half : 3 * half] = diagonal[half:, half:]

    @pl.when(band_ref[0] == 0)
    def _():
        out_ref[3 * half :] = dot(own, other_ref[:, :half], rows)

    @pl.when(band_ref[0] == 1)
    def _():
        out_ref[3 * half :] = dot(other_ref[...], own[:, half:], rows)


def sum_kernel(total, in_ref, out_ref):
    value = in_ref[0]
    for i in range(1, in_ref.shape[0]):
        value = value + in_ref[i]
    value = value / total
    for i in range(out_ref.shape[0]):
        out_ref[i] = value


def spread_row(value, row):
    return jnp.broadcast_to(value[row : row + 1, :], value.shape)


def inverse_factor(matrix, inverse):
    size = matrix.shape[0]
    tiles = PANEL // SUBLANES
    strips = size // LANES
    per_strip = LANES // PANEL
    sublane = lax.broadcasted_iota(jnp.int32, (SUBLANES, LANES), 0)
    lane = lax.broadcasted_iota(jnp.int32, (SUBLANES, LANES), 1)

    def step(p, carry):
        start = pl.multiple_of(p * PANEL, PANEL)
        strip = pl.multiple_of((p // per_strip) * LANES, LANES)
        shift = (p % per_strip) * PANEL
        block = pltpu.roll(matrix[pl.ds(start, PANEL), pl.ds(strip, LANES)], lax.rem(LANES - shift, LANES), 1)
        column = [
            [
                jnp.broadcast_to(block[SUBLANES * t : SUBLANES * (t + 1), j : j + 1], (SUBLANES, LANES))
                if t >= j // SUBLANES
                else None
                for t in range(tiles)
            ]
            for j in range(PANEL)
        ]
        rows = []
        for t in range(tiles):
            row = []
            for c in range(strips):
                value = matrix[pl.ds(start + SUBLANES * t, SUBLANES), LANES * c : LANES * (c + 1)]
                at = lane + (LANES * c - start)
                inside = (at >= 0) & (at < PANEL)
                row.append(jnp.where(inside, jnp.where(at == sublane + SUBLANES * t, 1.0, 0.0), value))
            rows.append(row)
        scales = [jnp.zeros((SUBLANES, LANES), jnp.float32) for _ in range(tiles)]
        for k in range(PANEL):
            tile, at = k // SUBLANES, k % SUBLANES
            pivot = spread_row(column[k][tile], at)
            scales[tile] = jnp.where(sublane == at, pivot, scales[tile])
            over = 1.0 / pivot
            factors = [None] * tiles
            for t in range(tile, tiles):
                factors[t] = column[k][t] * over
            factors[tile] = jnp.where(sublane > at, factors[tile], 0.0)
            for j in range(k + 1, PANEL):
                value = spread_row(column[k][j // SUBLANES], j % SUBLANES)
                for t in range(j // SUBLANES, tiles):
                    column[j][t] = column[j][t] - factors[t] * value
            for c in range(strips):
                value = spread_row(rows[tile][c], at)
                for t in range(tile, tiles):
                    rows[t][c] = rows[t][c] - factors[t] * value
        done = []
        for t in range(tiles):
            scale = lax.rsqrt(scales[t])
            done.append(jnp.concatenate([value * scale for value in rows[t]], axis=1))
        done = jnp.concatenate(done, axis=0)
        at = lax.broadcasted_iota(jnp.int32, done.shape, 1)
        inverse[pl.ds(start, PANEL), :] = jnp.where(at < start + PANEL, done, 0.0)
        below = jnp.where(at >= start + PANEL, done, 0.0)
        strip_at = lax.broadcasted_iota(jnp.int32, (LANES, size), 1)
        inside = (strip_at >= start) & (strip_at < start + PANEL)
        for r in range(strips):

            @pl.when(LANES * (r + 1) > start + PANEL)
            def _(r=r):
                update = dot(below[:, LANES * r : LANES * (r + 1)], done, ((0,), (0,)))
                old = matrix[LANES * r : LANES * (r + 1), :]
                matrix[LANES * r : LANES * (r + 1), :] = jnp.where(inside, 0.0, old) - update

        return carry

    lax.fori_loop(0, size // PANEL, step, 0)


def finish_kernel(band_ref, pieces_ref, own_ref, other_ref, out_ref, matrix, inverse):
    size = matrix.shape[0]
    block = own_ref.shape[1]
    half = block // 2
    bands = size // block
    rows = pieces_ref.shape[1]
    matrix[...] = jnp.zeros_like(matrix)
    for band in range(bands):
        spots = [
            (block * band, block * band),
            (block * band, block * band + half),
            (block * band + half, block * band + half),
            (0, block + half * band),
            (half, block + half * band),
        ]
        for r in range(0, 5 * half, SUBLANES):
            top, left = spots[r // half]
            top = top + r % half
            matrix[top : top + SUBLANES, left : left + half] = pieces_ref[
                (r // rows) * bands + band, r % rows : r % rows + SUBLANES, :
            ]
    inverse_factor(matrix, inverse)
    columns = ((1,), (1,))

    @pl.when(band_ref[0] == 0)
    def _():
        out_ref[...] = dot(own_ref[...], inverse[:block, :block], columns)

    @pl.when(band_ref[0] == 1)
    def _():
        out_ref[...] = dot(other_ref[...], inverse[block:, :block], columns) + dot(
            own_ref[...], inverse[block:, block:], columns
        )


def factor_kernel(in_ref, out_ref, matrix):
    matrix[...] = in_ref[...]
    inverse_factor(matrix, out_ref)


def call(kernel, shape, *args, scratch=(), scalars=0):
    specs = [pl.BlockSpec(memory_space=pltpu.SMEM)] * scalars + [VMEM] * (len(args) - scalars)
    return pl.pallas_call(
        kernel,
        out_shape=jax.ShapeDtypeStruct(shape, jnp.float32),
        in_specs=specs,
        out_specs=VMEM,
        scratch_shapes=list(scratch),
    )(*args)


def transposed(states, potential):
    size_x, size_y, nz, block = states.shape
    domains_y = lax.axis_size("dy")
    domains_x = lax.axis_size("dx")
    domains = domains_x * domains_y
    bands = lax.axis_size("band")
    cells = size_x * size_y * nz
    columns = size_x * size_y
    half = block // 2
    area = ("dx", "dy")
    everyone = ("dx", "dy", "band")
    band = lax.axis_index("band").astype(jnp.int32).reshape(1)

    packed = pl.pallas_call(
        functools.partial(pack_kernel, nz),
        out_shape=jax.ShapeDtypeStruct((domains, columns + size_y, LANES), jnp.float32),
        grid=(block // LANES,),
        in_specs=[
            pl.BlockSpec((cells, LANES), lambda i: (0, i)),
            pl.BlockSpec((size_x, size_y, nz), lambda i: (0, 0, 0)),
        ],
        out_specs=pl.BlockSpec((nz, columns + size_y, LANES), lambda i: (i, 0, 0)),
    )(states.reshape(cells, block), potential)
    packed = lax.all_to_all(packed, area, 0, 0, tiled=True)
    grid = (size_x * domains_x, size_y * domains_y, LANES)
    filtered = call(
        functools.partial(filter_kernel, nz, domains_y, size_x, size_y),
        (domains, columns, LANES),
        packed,
        scratch=[
            pltpu.VMEM((grid[0] + 2 * WIDTH,) + grid[1:], jnp.float32),
            pltpu.VMEM((3,) + grid, jnp.float32),
            pltpu.VMEM(grid, jnp.float32),
        ],
    )
    filtered = lax.all_to_all(filtered, area, 0, 0, tiled=True)
    own = pl.pallas_call(
        functools.partial(unpack_kernel, nz),
        out_shape=jax.ShapeDtypeStruct((cells, block), jnp.float32),
        grid=(block // LANES,),
        in_specs=[pl.BlockSpec((nz, columns, LANES), lambda i: (i, 0, 0))],
        out_specs=pl.BlockSpec((cells, LANES), lambda i: (0, i)),
    )(filtered)
    other = lax.ppermute(own, "band", [(0, 1), (1, 0)])
    partial = call(gram_kernel, (5 * half, half), band, own, other, scalars=1)
    partial = lax.all_to_all(partial.reshape(domains, 5 * half // domains, half), area, 0, 0, tiled=True)
    pieces = call(
        functools.partial(sum_kernel, float(cells * domains)),
        (domains * bands,) + partial.shape[1:],
        partial,
    )
    pieces = lax.all_to_all(pieces, everyone, 0, 0, tiled=True)
    size = block * bands
    result = call(
        finish_kernel,
        (cells, block),
        band,
        pieces,
        own,
        other,
        scratch=[pltpu.VMEM((size, size), jnp.float32)] * 2,
        scalars=1,
    )
    return result.reshape(states.shape)


def with_halo(cells, axis, dim, width):
    count = lax.axis_size(axis)
    size = cells.shape[dim]
    head = lax.slice_in_dim(cells, 0, width, axis=dim)
    tail = lax.slice_in_dim(cells, size - width, size, axis=dim)
    before = lax.ppermute(tail, axis, [(i, (i + 1) % count) for i in range(count)])
    after = lax.ppermute(head, axis, [((i + 1) % count, i) for i in range(count)])
    return jnp.concatenate([before, cells, after], axis=dim)


def apply_ham(field, potential):
    padded_x = with_halo(field, "dx", 0, WIDTH)
    padded_y = with_halo(field, "dy", 1, WIDTH)
    size_x = field.shape[0]
    size_y = field.shape[1]
    lap = 3.0 * coeffs[0] * field
    for shift in range(1, WIDTH + 1):
        near = (
            padded_x[WIDTH + shift : WIDTH + shift + size_x]
            + padded_x[WIDTH - shift : WIDTH - shift + size_x]
            + padded_y[:, WIDTH + shift : WIDTH + shift + size_y]
            + padded_y[:, WIDTH - shift : WIDTH - shift + size_y]
        )
        near = near + jnp.roll(field, shift, 2) + jnp.roll(field, -shift, 2)
        lap = lap + coeffs[shift] * near
    return -0.5 * lap + potential[..., None] * field


def haloed(states, potential):
    prev = states
    cur = (apply_ham(states, potential) - centre_value * states) / half_width
    for step in range(1, DEGREE):
        nxt = 2.0 * (apply_ham(cur, potential) - centre_value * cur) / half_width - prev
        prev, cur = (cur, nxt)
    block = cur.shape[3]
    cells = cur.shape[0] * cur.shape[1] * cur.shape[2]
    local = cur.reshape(cells, block)
    gathered = lax.all_gather(local, "band", axis=1, tiled=True)
    total = cells * lax.axis_size("dx") * lax.axis_size("dy")
    partial = jnp.dot(gathered.T, gathered, precision=HIGHEST, preferred_element_type=jnp.float32) / total
    correlation = lax.psum(partial, ("dx", "dy"))
    size = correlation.shape[0]
    if size % LANES == 0:
        inverse = call(factor_kernel, (size, size), correlation, scratch=[pltpu.VMEM((size, size), jnp.float32)])
    else:
        factor = jnp.linalg.cholesky(correlation)
        inverse = jax.scipy.linalg.solve_triangular(factor, jnp.eye(size, dtype=jnp.float32), lower=True)
    my_rows = lax.dynamic_slice_in_dim(inverse, lax.axis_index("band") * block, block, 0)
    result = jnp.dot(gathered, my_rows.T, precision=HIGHEST, preferred_element_type=jnp.float32)
    return result.reshape(cur.shape)


def shards(states, potential):
    size_x, size_y, nz, block = states.shape
    domains = lax.axis_size("dx") * lax.axis_size("dy")
    fits = (
        nz == SUBLANES
        and size_y == SUBLANES
        and nz * size_x <= LANES
        and block * nz == LANES * domains
        and block == 2 * LANES
        and lax.axis_size("band") == 2
        and (5 * LANES) % (domains * SUBLANES) == 0
        and lax.axis_size("dx") * size_x > 2 * WIDTH
        and lax.axis_size("dy") * size_y > 2 * WIDTH
    )
    return transposed(states, potential) if fits else haloed(states, potential)


def solution(mesh):
    return jax.shard_map(
        shards,
        mesh=mesh,
        in_specs=(P("dx", "dy", None, "band"), P("dx", "dy", None)),
        out_specs=P("dx", "dy", None, "band"),
        check_vma=False,
    )
```

time: 449 us -> 135 us (0.30); the launches traced: 443 us -> 134 us
  waiting for transfers between devices: 235 us -> 9.45 us
  other arithmetic: 128 us -> 0 us
  blocking collectives: 10.8 us -> 76.8 us
  Pallas kernels: 0 us -> 45.9 us
  local copies, waits for them, and re-layouts: 23.5 us -> 0.75 us
  between operations: 16.8 us -> 0.01 us
  matrix products: 15.7 us -> 0 us
  starting transfers between devices: 12 us -> 1.49 us
    ppermute x12 -> x1, waiting for transfers between devices: 143 us -> 9.45 us  [transposed(): other = lax.ppermute(own, 'band', [(0, 1), (1, 0)])]
    another operation x17 -> x0, other arithmetic: 120 us -> none  [the longest x14 78.9 us: shards(): factor = jnp.linalg.cholesky(correlation)]
    psum x1 -> x0, waiting for transfers between devices: 92.2 us -> none  [shards(): correlation = lax.psum(partial_gram, ('dx', 'dy'))]
    all_to_all x0 -> x4, blocking collectives: none -> 76.8 us  [the longest x1 22.5 us: transposed(): pieces = lax.all_to_all(pieces, everyone, 0, 0, tiled=True)]
    pallas_call x0 -> x6, Pallas kernels: none -> 45.9 us  [the longest x4 41.4 us: call(): pl.pallas_call(kernel, out_shape=jax.ShapeDtypeStruct(shape, jnp.float32)...]
    another operation x17 -> x0, local copies, waits for them, and re-layouts: 14.2 us -> none
    another operation x13 -> x0, matrix products: 11.1 us -> none  [the longest x7 5.67 us: shards(): inverse = jax.scipy.linalg.solve_triangular(factor, eye, lower=True)]
    all_gather x1 -> x0, blocking collectives: 10.8 us -> none  [shards(): gathered = lax.all_gather(local, 'band', axis=1, tiled=True)]
  transfers between devices with their start and end apart: 13 -> 1, of which waited for: 13 -> 1; matrix products, arithmetic and copies ran while one was open for 2% -> 0% of each run, Pallas kernels for 0% -> 0%
where the time goes in v1:
time: 135 us; the launch traced here: 134 us
  blocking collectives  76.8 us (57%)
  Pallas kernels  45.9 us (34%)
  waiting for transfers between devices  9.45 us (7%)
  starting transfers between devices  1.49 us (1%)
    pallas_call x4, Pallas kernels, call(): pl.pallas_call(kernel, out_shape=jax.ShapeDtypeStruct(shape, jnp.float32)...  41.4 us
    all_to_all x1, blocking collectives, transposed(): pieces = lax.all_to_all(pieces, everyone, 0, 0, tiled=True)  22.5 us
    all_to_all x1, blocking collectives, transposed(): packed = lax.all_to_all(packed, area, 0, 0, tiled=True)  21.7 us
    all_to_all x1, blocking collectives, transposed(): filtered = lax.all_to_all(filtered, area, 0, 0, tiled=True)  17 us
    all_to_all x1, blocking collectives, transposed(): lax.all_to_all(partial.reshape(domains, 5 * half // domains, half), area,...  15.6 us
    ppermute x1, waiting for transfers between devices, transposed(): other = lax.ppermute(own, 'band', [(0, 1), (1, 0)])  9.45 us
  transfers between devices with their start and end apart: 1, of which 1 were waited for; matrix products, arithmetic and copies ran while one was open for 0% of the time, Pallas kernels for 0%

profile of v1, /device:TPU:0, one launch (start us, length us, event | category | flops | bytes accessed | tf_op | source)
XLA Modules:
  0.0 134.3 jit_solution(10443546403804558907)
XLA Ops:
  0.0 2.3 %shard_map.28 = f32[16,56,128]{2,1,0:T(8,128)} custom-call(f32[384,256]{1,0:T(8,128)} %bitcast.5, f32[6,8,8]{2,1,0:T(8,128)} %potential_ref.1), custom_call_target="tpu_custom_call" | custom-call | tf_op jit(solution)/shard_map/pallas_call | solution.py:300
  2.3 21.7 %all_to_all.20.in_ref = f32[16,56,128]{2,1,0:T(8,128)} all-to-all(f32[16,56,128]{2,1,0:T(8,128)} %shard_map.28), channel_id=1, replica_groups=mesh['dx'=4,'dy'=4,'band'=2] {'dx','dy'}, dimensions={0} | all-to-all | bytes 917504 | tf_op jit(solution)/shard_map/all_to_all | solution.py:310
  23.9 7.1 %shard_map.29 = f32[16,48,128]{2,1,0:T(8,128)} custom-call(f32[16,56,128]{2,1,0:T(8,128)} %all_to_all.20.in_ref), custom_call_target="tpu_custom_call" | custom-call | tf_op jit(solution)/shard_map/pallas_call | solution.py:278
  31.1 17.0 %all_to_all.21.in_ref = f32[16,48,128]{2,1,0:T(8,128)} all-to-all(f32[16,48,128]{2,1,0:T(8,128)} %shard_map.29), channel_id=1, replica_groups=mesh['dx'=4,'dy'=4,'band'=2] {'dx','dy'}, dimensions={0} | all-to-all | bytes 786432 | tf_op jit(solution)/shard_map/all_to_all | solution.py:322
  48.1 2.2 %shard_map.30.own_ref = f32[384,256]{1,0:T(8,128)} custom-call(f32[16,48,128]{2,1,0:T(8,128)} %all_to_all.21.in_ref), custom_call_target="tpu_custom_call" | custom-call | tf_op jit(solution)/shard_map/pallas_call | solution.py:323
  50.3 1.5 %collective-permute-start = (f32[384,256]{1,0:T(8,128)}, f32[384,256]{1,0:T(8,128)S(1)}, u32[]{:S(2)}, u32[]{:S(2)}) collective-permute-start(f32[384,256]{1,0:T(8,128)} %shard_map.30.own_ref), channel_id=1, source_target_pairs={{0,1},{1,0},{2,3},{3,2},{4,5},{5,4},{6,7},{7,6},{8,9},{9,8},{10,11... | collective-permute-start | bytes 1179656 | tf_op jit(solution)/shard_map/ppermute | solution.py:330
  51.8 9.4 %collective-permute-done.other_ref = f32[384,256]{1,0:T(8,128)S(1)} collective-permute-done((f32[384,256]{1,0:T(8,128)}, f32[384,256]{1,0:T(8,128)S(1)}, u32[]{:S(2)}, u32[]{:S(2)}) %collective-permute-start) | collective-permute-done | bytes 393248 | tf_op jit(solution)/shard_map/ppermute | solution.py:330
  61.2 0.0 copy-start
  61.2 0.7 copy-done
  62.0 3.0 %shard_map.31 = f32[640,128]{1,0:T(8,128)} custom-call(s32[1]{0:T(128)} %bitcast.band_ref, f32[384,256]{1,0:T(8,128)} %shard_map.30.own_ref, f32[384,256]{1,0:T(8,128)} %copy-done), custom_call_target="tpu_custom_call" | custom-call | tf_op jit(solution)/shard_map/pallas_call | solution.py:278
  65.0 15.6 %all_to_all.22.in_ref = f32[16,40,128]{2,1,0:T(8,128)} all-to-all(f32[16,40,128]{2,1,0:T(8,128)} %bitcast.4), channel_id=1, replica_groups=mesh['dx'=4,'dy'=4,'band'=2] {'dx','dy'}, dimensions={0} | all-to-all | bytes 655360 | tf_op jit(solution)/shard_map/all_to_all | solution.py:332
  80.5 1.9 %shard_map.32 = f32[32,40,128]{2,1,0:T(8,128)} custom-call(f32[16,40,128]{2,1,0:T(8,128)} %all_to_all.22.in_ref), custom_call_target="tpu_custom_call" | custom-call | tf_op jit(solution)/shard_map/pallas_call | solution.py:278
  82.4 22.5 %all_to_all.23.pieces_ref = f32[32,40,128]{2,1,0:T(8,128)} all-to-all(f32[32,40,128]{2,1,0:T(8,128)} %shard_map.32), channel_id=1, replica_groups=mesh['dx'=4,'dy'=4,'band'=2] {'dx','dy','band'}, dimensions={0} | all-to-all | bytes 1310720 | tf_op jit(solution)/shard_map/all_to_all | solution.py:338
  104.9 29.4 %shard_map.33 = f32[384,256]{1,0:T(8,128)} custom-call(s32[1]{0:T(128)} %bitcast.band_ref, f32[32,40,128]{2,1,0:T(8,128)} %all_to_all.23.pieces_ref, f32[384,256]{1,0:T(8,128)} %shard_map.30.own_ref, f32[384,256]{1,0:T(8,128)} %copy-done), custom_call_target="tpu_custom_call" | custom-call | tf_op jit(solution)/shard_map/pallas_call | solution.py:278
Async XLA Ops:
  50.3 10.9 %collective-permute-start = (f32[384,256]{1,0:T(8,128)}, f32[384,256]{1,0:T(8,128)S(1)}, u32[]{:S(2)}, u32[]{:S(2)}) collective-permute-start(f32[384,256]{1,0:T(8,128)} %shard_map.30.own_ref), channel_id=1, source_target_pairs={{0,1},{1,0},{2,3},{3,2},{4,5},{5,4},{6,7},{7,6},{8,9},{9,8},{10,11... | collective-permute-start | bytes 1179656 | tf_op jit(solution)/shard_map/ppermute | solution.py:330
  61.2 0.7 copy-start

commit v2 on v1

--- a/solution.py
+++ b/solution.py
@@ -11,6 +11,7 @@
 LANES = 128
 SUBLANES = 8
 PANEL = 32
+PART = 16
 
 coeffs = (
     -5369.0 / 1800.0,
@@ -117,35 +118,35 @@
         if step + 1 < DEGREE:
             field[WIDTH : WIDTH + total_x] = spare[...]
 
+    shares = out_ref.shape[0] // domains
+    share = size_x // shares
     for i in range(domains):
         for x in range(size_x):
             at_x, at_y = place(i, x)
-            out_ref[i, size_y * x : size_y * (x + 1), :] = older[2, at_x, at_y : at_y + size_y, :]
-
-
-def unpack_kernel(nz, in_ref, out_ref):
+            row = size_y * (x % share)
+            out_ref[i * shares + x // share, row : row + size_y, :] = older[2, at_x, at_y : at_y + size_y, :]
+
+
+def upper_blocks(strips):
+    return [(i, j) for i in range(strips) for j in range(i, strips)]
+
+
+def gram_kernel(nz, bands, in_ref, cells_ref, out_ref):
     columns = in_ref.shape[1]
-    arrays = [in_ref[g] for g in range(nz)]
-    for z, value in enumerate(swap_groups(arrays, LANES // nz)):
-        out_ref[pl.ds(z, columns, stride=nz), :] = value
-
-
-def gram_kernel(band_ref, own_ref, other_ref, out_ref):
-    own = own_ref[...]
-    half = own.shape[1] // 2
-    rows = ((0,), (0,))
-    diagonal = dot(own, own, rows)
-    out_ref[0:half] = diagonal[:half, :half]
-    out_ref[half : 2 * half] = diagonal[:half, half:]
-    out_ref[2 * half : 3 * half] = diagonal[half:, half:]
-
-    @pl.when(band_ref[0] == 0)
-    def _():
-        out_ref[3 * half :] = dot(own, other_ref[:, :half], rows)
-
-    @pl.when(band_ref[0] == 1)
-    def _():
-        out_ref[3 * half :] = dot(other_ref[...], own[:, half:], rows)
+    strips = cells_ref.shape[0]
+    per_band = strips // bands
+    for strip in range(strips):
+        first = nz * (strip % per_band)
+        arrays = [in_ref[(first + g) * bands + strip // per_band] for g in range(nz)]
+        for z, value in enumerate(swap_groups(arrays, LANES // nz)):
+            cells_ref[strip, pl.ds(z, columns, stride=nz), :] = value
+    values = [cells_ref[strip] for strip in range(strips)]
+    at = 0
+    for i in range(strips):
+        product = dot(values[i], jnp.concatenate(values[i:], axis=1), ((0,), (0,)))
+        for j in range(strips - i):
+            out_ref[at : at + LANES, :] = product[:, LANES * j : LANES * (j + 1)]
+            at += LANES
 
 
 def sum_kernel(total, in_ref, out_ref):
@@ -161,116 +162,136 @@
     return jnp.broadcast_to(value[row : row + 1, :], value.shape)
 
 
-def inverse_factor(matrix, inverse):
-    size = matrix.shape[0]
+def split(value):
+    high = value.astype(jnp.bfloat16)
+    rest = value - high.astype(jnp.float32)
+    middle = rest.astype(jnp.bfloat16)
+    return high, middle, (rest - middle.astype(jnp.float32)).astype(jnp.bfloat16)
+
+
+def outer(left, right):
+    a, b, c = left
+    d, e, f = right
+    left = jnp.concatenate([a, a, b, b, a, c], axis=0)
+    right = jnp.concatenate([d, e, d, e, f, d], axis=0)
+    return lax.dot_general(left, right, (((0,), (0,)), ((), ())), preferred_element_type=jnp.float32)
+
+
+def eliminate(work, start):
     tiles = PANEL // SUBLANES
-    strips = size // LANES
-    per_strip = LANES // PANEL
+    strips = work.shape[1] // LANES
     sublane = lax.broadcasted_iota(jnp.int32, (SUBLANES, LANES), 0)
-    lane = lax.broadcasted_iota(jnp.int32, (SUBLANES, LANES), 1)
-
-    def step(p, carry):
-        start = pl.multiple_of(p * PANEL, PANEL)
-        strip = pl.multiple_of((p // per_strip) * LANES, LANES)
-        shift = (p % per_strip) * PANEL
-        block = pltpu.roll(matrix[pl.ds(start, PANEL), pl.ds(strip, LANES)], lax.rem(LANES - shift, LANES), 1)
-        column = [
-            [
-                jnp.broadcast_to(block[SUBLANES * t : SUBLANES * (t + 1), j : j + 1], (SUBLANES, LANES))
-                if t >= j // SUBLANES
-                else None
-                for t in range(tiles)
-            ]
-            for j in range(PANEL)
-        ]
-        rows = []
+    at = lax.broadcasted_iota(jnp.int32, (SUBLANES, LANES), 1) - start
+    rows = [
+        [work[start + SUBLANES * t : start + SUBLANES * (t + 1), LANES * c : LANES * (c + 1)] for c in range(strips)]
+        for t in range(tiles)
+    ]
+    pivots = [jnp.ones((SUBLANES, LANES), jnp.float32) for _ in range(tiles)]
+    for first in range(0, PANEL, PART):
+        column = {
+            (j, t): jnp.broadcast_to(rows[t][0][:, start + j : start + j + 1], (SUBLANES, LANES))
+            for j in range(first, first + PART)
+            for t in range(j // SUBLANES, tiles)
+        }
+        inside = (at >= first) & (at < first + PART)
         for t in range(tiles):
-            row = []
+            rows[t][0] = jnp.where(inside, jnp.where(at == sublane + SUBLANES * t, 1.0, 0.0), rows[t][0])
+        for k in range(first, first + PART):
+            tile, row = k // SUBLANES, k % SUBLANES
+            pivot = spread_row(column[k, tile], row)
+            pivots[tile] = jnp.where(sublane == row, pivot, pivots[tile])
+            over = 1.0 / pivot
+            factor = {t: column[k, t] * over for t in range(tile, tiles)}
+            factor[tile] = jnp.where(sublane > row, factor[tile], 0.0)
+            for j in range(k + 1, first + PART):
+                value = spread_row(column[k, j // SUBLANES], j % SUBLANES)
+                for t in range(j // SUBLANES, tiles):
+                    column[j, t] = column[j, t] - factor[t] * value
             for c in range(strips):
-                value = matrix[pl.ds(start + SUBLANES * t, SUBLANES), LANES * c : LANES * (c + 1)]
-                at = lane + (LANES * c - start)
-                inside = (at >= 0) & (at < PANEL)
-                row.append(jnp.where(inside, jnp.where(at == sublane + SUBLANES * t, 1.0, 0.0), value))
-            rows.append(row)
-        scales = [jnp.zeros((SUBLANES, LANES), jnp.float32) for _ in range(tiles)]
-        for k in range(PANEL):
-            tile, at = k // SUBLANES, k % SUBLANES
-            pivot = spread_row(column[k][tile], at)
-            scales[tile] = jnp.where(sublane == at, pivot, scales[tile])
-            over = 1.0 / pivot
-            factors = [None] * tiles
-            for t in range(tile, tiles):
-                factors[t] = column[k][t] * over
-            factors[tile] = jnp.where(sublane > at, factors[tile], 0.0)
-            for j in range(k + 1, PANEL):
-                value = spread_row(column[k][j // SUBLANES], j % SUBLANES)
-                for t in range(j // SUBLANES, tiles):
-                    column[j][t] = column[j][t] - factors[t] * value
-            for c in range(strips):
-                value = spread_row(rows[tile][c], at)
+                value = spread_row(rows[tile][c], row)
                 for t in range(tile, tiles):
-                    rows[t][c] = rows[t][c] - factors[t] * value
-        done = []
-        for t in range(tiles):
-            scale = lax.rsqrt(scales[t])
-            done.append(jnp.concatenate([value * scale for value in rows[t]], axis=1))
-        done = jnp.concatenate(done, axis=0)
-        at = lax.broadcasted_iota(jnp.int32, done.shape, 1)
-        inverse[pl.ds(start, PANEL), :] = jnp.where(at < start + PANEL, done, 0.0)
-        below = jnp.where(at >= start + PANEL, done, 0.0)
-        strip_at = lax.broadcasted_iota(jnp.int32, (LANES, size), 1)
-        inside = (strip_at >= start) & (strip_at < start + PANEL)
-        for r in range(strips):
-
-            @pl.when(LANES * (r + 1) > start + PANEL)
-            def _(r=r):
-                update = dot(below[:, LANES * r : LANES * (r + 1)], done, ((0,), (0,)))
-                old = matrix[LANES * r : LANES * (r + 1), :]
-                matrix[LANES * r : LANES * (r + 1), :] = jnp.where(inside, 0.0, old) - update
+                    rows[t][c] = rows[t][c] - factor[t] * value
+    scaled = [jnp.concatenate([v * lax.rsqrt(pivots[t]) for v in rows[t]], axis=1) for t in range(tiles)]
+    return jnp.concatenate(scaled, axis=0)
+
+
+def inverse_factor(matrix, inverse, work, done):
+    strips = matrix.shape[0] // LANES
+
+    def step(block, carry):
+        base = pl.multiple_of(block * LANES, LANES)
+        strip = [pl.multiple_of(lax.rem(block + c, strips) * LANES, LANES) for c in range(strips)]
+        for c in range(strips):
+            work[:, LANES * c : LANES * (c + 1)] = matrix[pl.ds(base, LANES), pl.ds(strip[c], LANES)]
+        for start in range(0, LANES, PANEL):
+            end = start + PANEL
+            value = eliminate(work, start)
+            lane = lax.broadcasted_iota(jnp.int32, (PANEL, LANES), 1)
+            done[start:end, :LANES] = jnp.where(lane < end, value[:, :LANES], 0.0)
+            done[start:end, LANES:] = value[:, LANES:]
+            if end < LANES:
+                parts = split(value)
+                update = outer([part[:, :LANES] for part in parts], parts)
+                lane = lax.broadcasted_iota(jnp.int32, (LANES - end, LANES), 1)
+                old = jnp.where((lane >= start) & (lane < end), 0.0, work[end:, :LANES])
+                work[end:, :LANES] = old - update[end:, :LANES]
+                work[end:, LANES:] = work[end:, LANES:] - update[end:, LANES:]
+        inverse[pl.ds(base, LANES), pl.ds(strip[0], LANES)] = done[:, :LANES]
+        for c in range(1, strips):
+            value = jnp.where(block + c >= strips, done[:, LANES * c : LANES * (c + 1)], 0.0)
+            inverse[pl.ds(base, LANES), pl.ds(strip[c], LANES)] = value
+
+        @pl.when(block + 1 < strips)
+        def _():
+            parts = split(done[...])
+            for c in range(1, strips):
+
+                @pl.when(block + c < strips)
+                def _(c=c):
+                    update = outer([part[:, LANES * c : LANES * (c + 1)] for part in parts], parts)
+                    rows = pl.ds(pl.multiple_of((block + c) * LANES, LANES), LANES)
+                    matrix[rows, pl.ds(strip[0], LANES)] = -update[:, :LANES]
+                    for e in range(1, strips):
+                        columns = pl.ds(strip[e], LANES)
+                        matrix[rows, columns] = matrix[rows, columns] - update[:, LANES * e : LANES * (e + 1)]
 
         return carry
 
-    lax.fori_loop(0, size // PANEL, step, 0)
-
-
-def finish_kernel(band_ref, pieces_ref, own_ref, other_ref, out_ref, matrix, inverse):
-    size = matrix.shape[0]
-    block = own_ref.shape[1]
-    half = block // 2
-    bands = size // block
+    lax.fori_loop(0, strips, step, 0)
+
+
+def finish_kernel(band_ref, pieces_ref, own_ref, other_ref, out_ref, matrix, inverse, work, done):
+    strips = own_ref.shape[0]
+    cells = own_ref.shape[1]
+    block = out_ref.shape[1]
     rows = pieces_ref.shape[1]
     matrix[...] = jnp.zeros_like(matrix)
-    for band in range(bands):
-        spots = [
-            (block * band, block * band),
-            (block * band, block * band + half),
-            (block * band + half, block * band + half),
-            (0, block + half * band),
-            (half, block + half * band),
-        ]
-        for r in range(0, 5 * half, SUBLANES):
-            top, left = spots[r // half]
-            top = top + r % half
-            matrix[top : top + SUBLANES, left : left + half] = pieces_ref[
-                (r // rows) * bands + band, r % rows : r % rows + SUBLANES, :
+    for at, (i, j) in enumerate(upper_blocks(strips)):
+        for r in range(0, LANES, SUBLANES):
+            from_row = LANES * at + r
+            matrix[LANES * i + r : LANES * i + r + SUBLANES, LANES * j : LANES * (j + 1)] = pieces_ref[
+                from_row // rows, from_row % rows : from_row % rows + SUBLANES, :
             ]
-    inverse_factor(matrix, inverse)
-    columns = ((1,), (1,))
-
-    @pl.when(band_ref[0] == 0)
-    def _():
-        out_ref[...] = dot(own_ref[...], inverse[:block, :block], columns)
-
-    @pl.when(band_ref[0] == 1)
-    def _():
-        out_ref[...] = dot(other_ref[...], inverse[block:, :block], columns) + dot(
-            own_ref[...], inverse[block:, block:], columns
-        )
-
-
-def factor_kernel(in_ref, out_ref, matrix):
+    inverse_factor(matrix, inverse, work, done)
+    band = band_ref[0]
+    for b in range(strips * LANES // block):
+
+        @pl.when(band == b)
+        def _(b=b):
+            used = block * (b + 1)
+            mine = inverse[block * b : used, :used]
+            for share, ref in ((b, own_ref), (1 - b, other_ref)):
+                value = jnp.concatenate([ref[s] for s in range(used // LANES)], axis=1)
+                out_ref[cells * share : cells * (share + 1), :] = dot(value, mine, ((1,), (1,)))
+
+
+def factor_kernel(in_ref, out_ref, matrix, work, done):
     matrix[...] = in_ref[...]
-    inverse_factor(matrix, out_ref)
+    inverse_factor(matrix, out_ref, work, done)
+
+
+def factor_scratch(size):
+    return [pltpu.VMEM((rows, size), jnp.float32) for rows in (size, LANES, LANES)]
 
 
 def call(kernel, shape, *args, scratch=(), scalars=0):
@@ -292,7 +313,6 @@
     bands = lax.axis_size("band")
     cells = size_x * size_y * nz
     columns = size_x * size_y
-    half = block // 2
     area = ("dx", "dy")
     everyone = ("dx", "dy", "band")
     band = lax.axis_index("band").astype(jnp.int32).reshape(1)
@@ -311,7 +331,7 @@
     grid = (size_x * domains_x, size_y * domains_y, LANES)
     filtered = call(
         functools.partial(filter_kernel, nz, domains_y, size_x, size_y),
-        (domains, columns, LANES),
+        (domains * bands, columns // bands, LANES),
         packed,
         scratch=[
             pltpu.VMEM((grid[0] + 2 * WIDTH,) + grid[1:], jnp.float32),
@@ -319,24 +339,24 @@
             pltpu.VMEM(grid, jnp.float32),
         ],
     )
-    filtered = lax.all_to_all(filtered, area, 0, 0, tiled=True)
-    own = pl.pallas_call(
-        functools.partial(unpack_kernel, nz),
-        out_shape=jax.ShapeDtypeStruct((cells, block), jnp.float32),
-        grid=(block // LANES,),
-        in_specs=[pl.BlockSpec((nz, columns, LANES), lambda i: (i, 0, 0))],
-        out_specs=pl.BlockSpec((cells, LANES), lambda i: (0, i)),
+    filtered = lax.all_to_all(filtered, everyone, 0, 0, tiled=True)
+    size = block * bands
+    strips = size // LANES
+    rows = len(upper_blocks(strips)) * LANES
+    own, partial = pl.pallas_call(
+        functools.partial(gram_kernel, nz, bands),
+        out_shape=(
+            jax.ShapeDtypeStruct((strips, cells // bands, LANES), jnp.float32),
+            jax.ShapeDtypeStruct((rows, LANES), jnp.float32),
+        ),
+        in_specs=[VMEM],
+        out_specs=(VMEM, VMEM),
     )(filtered)
     other = lax.ppermute(own, "band", [(0, 1), (1, 0)])
-    partial = call(gram_kernel, (5 * half, half), band, own, other, scalars=1)
-    partial = lax.all_to_all(partial.reshape(domains, 5 * half // domains, half), area, 0, 0, tiled=True)
-    pieces = call(
-        functools.partial(sum_kernel, float(cells * domains)),
-        (domains * bands,) + partial.shape[1:],
-        partial,
-    )
+    devices = domains * bands
+    partial = lax.all_to_all(partial.reshape(devices, rows // devices, LANES), everyone, 0, 0, tiled=True)
+    pieces = call(functools.partial(sum_kernel, float(cells * domains)), partial.shape, partial)
     pieces = lax.all_to_all(pieces, everyone, 0, 0, tiled=True)
-    size = block * bands
     result = call(
         finish_kernel,
         (cells, block),
@@ -344,7 +364,7 @@
         pieces,
         own,
         other,
-        scratch=[pltpu.VMEM((size, size), jnp.float32)] * 2,
+        scratch=[pltpu.VMEM((size, size), jnp.float32)] + factor_scratch(size),
         scalars=1,
     )
     return result.reshape(states.shape)
@@ -393,7 +413,7 @@
     correlation = lax.psum(partial, ("dx", "dy"))
     size = correlation.shape[0]
     if size % LANES == 0:
-        inverse = call(factor_kernel, (size, size), correlation, scratch=[pltpu.VMEM((size, size), jnp.float32)])
+        inverse = call(factor_kernel, (size, size), correlation, scratch=factor_scratch(size))
     else:
         factor = jnp.linalg.cholesky(correlation)
         inverse = jax.scipy.linalg.solve_triangular(factor, jnp.eye(size, dtype=jnp.float32), lower=True)
@@ -412,7 +432,8 @@
         and block * nz == LANES * domains
         and block == 2 * LANES
         and lax.axis_size("band") == 2
-        and (5 * LANES) % (domains * SUBLANES) == 0
+        and size_x % 2 == 0
+        and (10 * LANES) % (2 * domains * SUBLANES) == 0
         and lax.axis_size("dx") * size_x > 2 * WIDTH
         and lax.axis_size("dy") * size_y > 2 * WIDTH
     )

time: 135 us -> 116 us (0.86)
  blocking collectives: 76.8 us -> 60.9 us
  Pallas kernels: 45.9 us -> 31.3 us
  waiting for transfers between devices: 9.45 us -> 17.3 us
  starting transfers between devices: 1.49 us -> 4.45 us
    all_to_all x3 -> x2, blocking collectives: 55.1 us -> 39.3 us  [the longest x1 22.4 us: transposed(): lax.all_to_all(partial.reshape(devices, rows // devices, LANES), everyone...]
    pallas_call x4 -> x3, Pallas kernels: 41.4 us -> 26 us  [call(): pl.pallas_call(kernel, out_shape=jax.ShapeDtypeStruct(shape, jnp.float32)...]
    ppermute x1, waiting for transfers between devices: 9.45 us -> 16.1 us  [transposed(): other = lax.ppermute(own, 'band', [(0, 1), (1, 0)])]
    all_to_all x0 -> x1, starting transfers between devices: none -> 2.75 us  [transposed(): pieces = lax.all_to_all(pieces, everyone, 0, 0, tiled=True)]
  transfers between devices with their start and end apart: 1 -> 2, of which waited for: 1 -> 2; matrix products, arithmetic and copies ran while one was open for 0% -> 0% of each run, Pallas kernels for 0% -> 0%
where the time goes in v2:
time: 116 us; the launch traced here: 115 us
  blocking collectives  60.9 us (52%)
  Pallas kernels  31.3 us (27%)
  waiting for transfers between devices  17.3 us (15%)
  starting transfers between devices  4.45 us (4%)
    pallas_call x3, Pallas kernels, call(): pl.pallas_call(kernel, out_shape=jax.ShapeDtypeStruct(shape, jnp.float32)...  26 us
    all_to_all x1, blocking collectives, transposed(): lax.all_to_all(partial.reshape(devices, rows // devices, LANES), everyone...  22.4 us
    all_to_all x1, blocking collectives, transposed(): packed = lax.all_to_all(packed, area, 0, 0, tiled=True)  21.7 us
    all_to_all x1, blocking collectives, transposed(): filtered = lax.all_to_all(filtered, everyone, 0, 0, tiled=True)  16.9 us
    ppermute x1, waiting for transfers between devices, transposed(): other = lax.ppermute(own, 'band', [(0, 1), (1, 0)])  16.1 us
    pallas_call x1, Pallas kernels, transposed(): pl.pallas_call(functools.partial(gram_kernel, nz, bands), out_shape=(jax....  3.03 us
    all_to_all x1, starting transfers between devices, transposed(): pieces = lax.all_to_all(pieces, everyone, 0, 0, tiled=True)  2.75 us
  transfers between devices with their start and end apart: 2, of which 2 were waited for; matrix products, arithmetic and copies ran while one was open for 0% of the time, Pallas kernels for 0%

profile of v2, /device:TPU:0, one launch (start us, length us, event | category | flops | bytes accessed | tf_op | source)
XLA Modules:
  0.0 114.9 jit_solution(3956813469506118476)
XLA Ops:
  0.0 2.3 %shard_map.28 = f32[16,56,128]{2,1,0:T(8,128)} custom-call(f32[384,256]{1,0:T(8,128)} %bitcast.5, f32[6,8,8]{2,1,0:T(8,128)} %potential_ref.1), custom_call_target="tpu_custom_call" | custom-call | tf_op jit(solution)/shard_map/pallas_call | solution.py:320
  2.3 21.7 %all_to_all.20.in_ref = f32[16,56,128]{2,1,0:T(8,128)} all-to-all(f32[16,56,128]{2,1,0:T(8,128)} %shard_map.28), channel_id=1, replica_groups=mesh['dx'=4,'dy'=4,'band'=2] {'dx','dy'}, dimensions={0} | all-to-all | bytes 917504 | tf_op jit(solution)/shard_map/all_to_all | solution.py:330
  23.9 7.1 %shard_map.29 = f32[32,24,128]{2,1,0:T(8,128)} custom-call(f32[16,56,128]{2,1,0:T(8,128)} %all_to_all.20.in_ref), custom_call_target="tpu_custom_call" | custom-call | tf_op jit(solution)/shard_map/pallas_call | solution.py:299
  31.1 16.9 %all_to_all.21.in_ref = f32[32,24,128]{2,1,0:T(8,128)} all-to-all(f32[32,24,128]{2,1,0:T(8,128)} %shard_map.29), channel_id=1, replica_groups=mesh['dx'=4,'dy'=4,'band'=2] {'dx','dy','band'}, dimensions={0} | all-to-all | bytes 786432 | tf_op jit(solution)/shard_map/all_to_all | solution.py:342
  48.0 3.0 %shard_map.30 = (f32[4,192,128]{2,1,0:T(8,128)}, f32[1280,128]{1,0:T(8,128)}) custom-call(f32[32,24,128]{2,1,0:T(8,128)} %all_to_all.21.in_ref), custom_call_target="tpu_custom_call" | custom-call | tf_op jit(solution)/shard_map/pallas_call | solution.py:346
  51.0 22.4 %all_to_all.22.in_ref = f32[32,40,128]{2,1,0:T(8,128)} all-to-all(f32[32,40,128]{2,1,0:T(8,128)} %bitcast.4), channel_id=1, replica_groups=mesh['dx'=4,'dy'=4,'band'=2] {'dx','dy','band'}, dimensions={0} | all-to-all | bytes 1310720 | tf_op jit(solution)/shard_map/all_to_all | solution.py:357
  73.4 2.0 %shard_map.31 = f32[32,40,128]{2,1,0:T(8,128)} custom-call(f32[32,40,128]{2,1,0:T(8,128)} %all_to_all.22.in_ref), custom_call_target="tpu_custom_call" | custom-call | tf_op jit(solution)/shard_map/pallas_call | solution.py:299
  75.4 0.0 copy-start.1
  75.4 2.7 %all-to-all-start.3 = ((f32[32,40,128]{2,1,0:T(8,128)}), f32[32,40,128]{2,1,0:T(8,128)S(1)}, u32[]{:S(2)}, u32[]{:S(2)}) async-start(f32[32,40,128]{2,1,0:T(8,128)} %shard_map.31), calls=%async_computation.3 | async-start | bytes 1310720 | tf_op jit(solution)/shard_map/all_to_all | solution.py:359
  78.1 0.0 copy-done.1
  78.1 1.7 %collective-permute-start = (f32[4,192,128]{2,1,0:T(8,128)S(1)}, f32[4,192,128]{2,1,0:T(8,128)S(1)}, u32[]{:S(2)}, u32[]{:S(2)}) collective-permute-start(f32[4,192,128]{2,1,0:T(8,128)S(1)} %copy-done.1), channel_id=1, source_target_pairs={{0,1},{1,0},{2,3},{3,2},{4,5},{5,4},{6,7},{7,6},{8,9},{9,8},{10,11... | collective-permute-start | bytes 1179656 | tf_op jit(solution)/shard_map/ppermute | solution.py:355
  79.8 16.1 %collective-permute-done.other_ref = f32[4,192,128]{2,1,0:T(8,128)S(1)} collective-permute-done((f32[4,192,128]{2,1,0:T(8,128)S(1)}, f32[4,192,128]{2,1,0:T(8,128)S(1)}, u32[]{:S(2)}, u32[]{:S(2)}) %collective-permute-start) | collective-permute-done | bytes 393248 | tf_op jit(solution)/shard_map/ppermute | solution.py:355
  95.9 0.0 copy-start.2
  95.9 1.3 %all-to-all-done.3.pieces_ref = f32[32,40,128]{2,1,0:T(8,128)S(1)} async-done(((f32[32,40,128]{2,1,0:T(8,128)}), f32[32,40,128]{2,1,0:T(8,128)S(1)}, u32[]{:S(2)}, u32[]{:S(2)}) %all-to-all-start.3) | async-done | bytes 655392 | tf_op jit(solution)/shard_map/all_to_all | solution.py:359
  97.2 0.0 copy-start
  97.2 0.0 copy-done.2
  97.2 0.8 copy-done
  98.0 16.9 %shard_map.32 = f32[384,256]{1,0:T(8,128)} custom-call(s32[1]{0:T(128)} %bitcast.band_ref, f32[32,40,128]{2,1,0:T(8,128)} %copy-done, f32[4,192,128]{2,1,0:T(8,128)} %get-tuple-element.8.own_ref, f32[4,192,128]{2,1,0:T(8,128)} %copy-done.2), custom_call_target="tpu_custom_call" | custom-call | tf_op jit(solution)/shard_map/pallas_call | solution.py:299
Async XLA Ops:
  75.4 2.8 %copy-start.1 = (f32[4,192,128]{2,1,0:T(8,128)S(1)}, f32[4,192,128]{2,1,0:T(8,128)}, u32[]{:S(2)}) copy-start(f32[4,192,128]{2,1,0:T(8,128)} %get-tuple-element.8.own_ref) | copy-start | bytes 1179652
  75.4 21.8 %all-to-all-start.3 = ((f32[32,40,128]{2,1,0:T(8,128)}), f32[32,40,128]{2,1,0:T(8,128)S(1)}, u32[]{:S(2)}, u32[]{:S(2)}) async-start(f32[32,40,128]{2,1,0:T(8,128)} %shard_map.31), calls=%async_computation.3 | async-start | bytes 1310720 | tf_op jit(solution)/shard_map/all_to_all | solution.py:359
  78.1 17.8 %collective-permute-start = (f32[4,192,128]{2,1,0:T(8,128)S(1)}, f32[4,192,128]{2,1,0:T(8,128)S(1)}, u32[]{:S(2)}, u32[]{:S(2)}) collective-permute-start(f32[4,192,128]{2,1,0:T(8,128)S(1)} %copy-done.1), channel_id=1, source_target_pairs={{0,1},{1,0},{2,3},{3,2},{4,5},{5,4},{6,7},{7,6},{8,9},{9,8},{10,11... | collective-permute-start | bytes 1179656 | tf_op jit(solution)/shard_map/ppermute | solution.py:355
  95.9 1.3 %copy-start.2 = (f32[4,192,128]{2,1,0:T(8,128)}, f32[4,192,128]{2,1,0:T(8,128)S(1)}, u32[]{:S(2)}) copy-start(f32[4,192,128]{2,1,0:T(8,128)S(1)} %collective-permute-done.other_ref) | copy-start | bytes 1179652
  97.2 0.8 copy-start

commit v3 on v2

--- a/solution.py
+++ b/solution.py
@@ -12,6 +12,7 @@
 SUBLANES = 8
 PANEL = 32
 PART = 16
+CORES = 2
 
 coeffs = (
     -5369.0 / 1800.0,
@@ -26,6 +27,7 @@
 half_width = 5.0
 centre_value = 7.0
 VMEM = pl.BlockSpec(memory_space=pltpu.VMEM)
+SMEM = pl.BlockSpec(memory_space=pltpu.SMEM)
 HIGHEST = lax.Precision.HIGHEST
 
 
@@ -131,22 +133,27 @@
     return [(i, j) for i in range(strips) for j in range(i, strips)]
 
 
-def gram_kernel(nz, bands, in_ref, cells_ref, out_ref):
-    columns = in_ref.shape[1]
-    strips = cells_ref.shape[0]
+def share_of(strips, core):
+    return upper_blocks(strips)[core :: CORES]
+
+
+def gram_kernel(nz, bands, core_ref, own_ref, other_ref, cells_ref, out_ref, paired):
+    columns = own_ref.shape[1]
+    strips, rows, _ = cells_ref.shape
     per_band = strips // bands
     for strip in range(strips):
         first = nz * (strip % per_band)
-        arrays = [in_ref[(first + g) * bands + strip // per_band] for g in range(nz)]
-        for z, value in enumerate(swap_groups(arrays, LANES // nz)):
-            cells_ref[strip, pl.ds(z, columns, stride=nz), :] = value
-    values = [cells_ref[strip] for strip in range(strips)]
-    at = 0
-    for i in range(strips):
-        product = dot(values[i], jnp.concatenate(values[i:], axis=1), ((0,), (0,)))
-        for j in range(strips - i):
-            out_ref[at : at + LANES, :] = product[:, LANES * j : LANES * (j + 1)]
-            at += LANES
+        for half, ref in enumerate((own_ref, other_ref)):
+            arrays = [ref[(first + g) * bands + strip // per_band] for g in range(nz)]
+            for z, value in enumerate(swap_groups(arrays, LANES // nz)):
+                paired[strip, pl.ds(half * rows + z, columns, stride=nz), :] = value
+        cells_ref[strip] = paired[strip, :rows, :]
+    for core in range(CORES):
+
+        @pl.when(core_ref[0] == core)
+        def _(core=core):
+            for at, (i, j) in enumerate(share_of(strips, core)):
+                out_ref[LANES * at : LANES * (at + 1), :] = dot(paired[i], paired[j], ((0,), (0,)))
 
 
 def sum_kernel(total, in_ref, out_ref):
@@ -260,20 +267,25 @@
     lax.fori_loop(0, strips, step, 0)
 
 
-def finish_kernel(band_ref, pieces_ref, own_ref, other_ref, out_ref, matrix, inverse, work, done):
+def finish_kernel(place_ref, mine_ref, theirs_ref, own_ref, other_ref, out_ref, matrix, inverse, work, done):
     strips = own_ref.shape[0]
     cells = own_ref.shape[1]
     block = out_ref.shape[1]
-    rows = pieces_ref.shape[1]
+    rows = mine_ref.shape[1]
     matrix[...] = jnp.zeros_like(matrix)
-    for at, (i, j) in enumerate(upper_blocks(strips)):
-        for r in range(0, LANES, SUBLANES):
-            from_row = LANES * at + r
-            matrix[LANES * i + r : LANES * i + r + SUBLANES, LANES * j : LANES * (j + 1)] = pieces_ref[
-                from_row // rows, from_row % rows : from_row % rows + SUBLANES, :
-            ]
+    for core in range(CORES):
+
+        @pl.when(place_ref[0] == core)
+        def _(core=core):
+            for ref, holder in ((mine_ref, core), (theirs_ref, 1 - core)):
+                for at, (i, j) in enumerate(share_of(strips, holder)):
+                    for r in range(0, LANES, SUBLANES):
+                        piece, row = divmod(LANES * at + r, rows)
+                        top, left = LANES * i + r, LANES * j
+                        matrix[top : top + SUBLANES, left : left + LANES] = ref[piece, row : row + SUBLANES, :]
+
     inverse_factor(matrix, inverse, work, done)
-    band = band_ref[0]
+    band = place_ref[1]
     for b in range(strips * LANES // block):
 
         @pl.when(band == b)
@@ -295,7 +307,7 @@
 
 
 def call(kernel, shape, *args, scratch=(), scalars=0):
-    specs = [pl.BlockSpec(memory_space=pltpu.SMEM)] * scalars + [VMEM] * (len(args) - scalars)
+    specs = [SMEM] * scalars + [VMEM] * (len(args) - scalars)
     return pl.pallas_call(
         kernel,
         out_shape=jax.ShapeDtypeStruct(shape, jnp.float32),
@@ -308,14 +320,16 @@
 def transposed(states, potential):
     size_x, size_y, nz, block = states.shape
     domains_y = lax.axis_size("dy")
-    domains_x = lax.axis_size("dx")
+    domains_x = lax.axis_size("chip") * CORES
     domains = domains_x * domains_y
     bands = lax.axis_size("band")
     cells = size_x * size_y * nz
     columns = size_x * size_y
-    area = ("dx", "dy")
-    everyone = ("dx", "dy", "band")
-    band = lax.axis_index("band").astype(jnp.int32).reshape(1)
+    area = ("chip", "core", "dy")
+    everyone = area + ("band",)
+    same_core = ("chip", "dy", "band")
+    swap = [(0, 1), (1, 0)]
+    place = jnp.stack([lax.axis_index("core"), lax.axis_index("band")]).astype(jnp.int32)
 
     packed = pl.pallas_call(
         functools.partial(pack_kernel, nz),
@@ -342,26 +356,30 @@
     filtered = lax.all_to_all(filtered, everyone, 0, 0, tiled=True)
     size = block * bands
     strips = size // LANES
-    rows = len(upper_blocks(strips)) * LANES
+    rows = len(share_of(strips, 0)) * LANES
+    holders = domains * bands // CORES
+    neighbours = lax.ppermute(filtered, "core", swap)
     own, partial = pl.pallas_call(
         functools.partial(gram_kernel, nz, bands),
         out_shape=(
             jax.ShapeDtypeStruct((strips, cells // bands, LANES), jnp.float32),
             jax.ShapeDtypeStruct((rows, LANES), jnp.float32),
         ),
-        in_specs=[VMEM],
+        in_specs=[SMEM, VMEM, VMEM],
         out_specs=(VMEM, VMEM),
-    )(filtered)
-    other = lax.ppermute(own, "band", [(0, 1), (1, 0)])
-    devices = domains * bands
-    partial = lax.all_to_all(partial.reshape(devices, rows // devices, LANES), everyone, 0, 0, tiled=True)
+        scratch_shapes=[pltpu.VMEM((strips, CORES * cells // bands, LANES), jnp.float32)],
+    )(place, filtered, neighbours)
+    other = lax.ppermute(own, "band", swap)
+    partial = lax.all_to_all(partial.reshape(holders, rows // holders, LANES), same_core, 0, 0, tiled=True)
     pieces = call(functools.partial(sum_kernel, float(cells * domains)), partial.shape, partial)
-    pieces = lax.all_to_all(pieces, everyone, 0, 0, tiled=True)
+    mine = lax.all_to_all(pieces, same_core, 0, 0, tiled=True)
+    theirs = lax.ppermute(mine, "core", swap)
     result = call(
         finish_kernel,
         (cells, block),
-        band,
-        pieces,
+        place,
+        mine,
+        theirs,
         own,
         other,
         scratch=[pltpu.VMEM((size, size), jnp.float32)] + factor_scratch(size),
@@ -422,29 +440,34 @@
     return result.reshape(cur.shape)
 
 
-def shards(states, potential):
-    size_x, size_y, nz, block = states.shape
-    domains = lax.axis_size("dx") * lax.axis_size("dy")
-    fits = (
-        nz == SUBLANES
-        and size_y == SUBLANES
-        and nz * size_x <= LANES
-        and block * nz == LANES * domains
-        and block == 2 * LANES
-        and lax.axis_size("band") == 2
-        and size_x % 2 == 0
-        and (10 * LANES) % (2 * domains * SUBLANES) == 0
-        and lax.axis_size("dx") * size_x > 2 * WIDTH
-        and lax.axis_size("dy") * size_y > 2 * WIDTH
-    )
-    return transposed(states, potential) if fits else haloed(states, potential)
-
-
 def solution(mesh):
-    return jax.shard_map(
-        shards,
-        mesh=mesh,
-        in_specs=(P("dx", "dy", None, "band"), P("dx", "dy", None)),
-        out_specs=P("dx", "dy", None, "band"),
-        check_vma=False,
-    )
+    domains_x, domains_y, bands = (mesh.shape[name] for name in ("dx", "dy", "band"))
+    domains = domains_x * domains_y
+
+    def run(states, potential):
+        total_x, total_y, nz, size = states.shape
+        size_x, size_y, block = total_x // domains_x, total_y // domains_y, size // bands
+        if (
+            nz == SUBLANES
+            and size_y == SUBLANES
+            and nz * size_x <= LANES
+            and block * nz == LANES * domains
+            and block % LANES == 0
+            and bands == 2
+            and size_x % bands == 0
+            and domains_x % CORES == 0
+            and (size // LANES) * (size // LANES + 1) * LANES % (2 * domains * bands * SUBLANES) == 0
+            and total_x > 2 * WIDTH
+            and total_y > 2 * WIDTH
+        ):
+            devices = mesh.devices.reshape(domains_x // CORES, CORES, domains_y, bands)
+            body, over = transposed, jax.sharding.Mesh(devices, ("chip", "core", "dy", "band"))
+            x_axis = ("chip", "core")
+        else:
+            body, over, x_axis = haloed, mesh, "dx"
+        spec = P(x_axis, "dy", None, "band")
+        return jax.shard_map(
+            body, mesh=over, in_specs=(spec, P(x_axis, "dy", None)), out_specs=spec, check_vma=False
+        )(states, potential)
+
+    return run

time: 116 us -> 109 us (0.940)
  blocking collectives: 60.9 us -> 54.6 us
  waiting for transfers between devices: 17.3 us -> 12.7 us
  local copies, waits for them, and re-layouts: 0.84 us -> 2.24 us
    ppermute x1 -> x3, waiting for transfers between devices: 16.1 us -> 3.98 us  [the longest x1 2.87 us: transposed(): other = lax.ppermute(own, 'band', swap)]
    all_to_all x1, waiting for transfers between devices: 1.28 us -> 8.7 us  [transposed(): mine = lax.all_to_all(pieces, same_core, 0, 0, tiled=True)]
    all_to_all x1, blocking collectives: 22.4 us -> 16.1 us  [transposed(): lax.all_to_all(partial.reshape(holders, rows // holders, LANES), same_cor...]
    unnamed x6 -> x12, local copies, waits for them, and re-layouts: 0.84 us -> 2.24 us
    pallas_call x1, Pallas kernels: 3.03 us -> 4.35 us  [transposed(): pl.pallas_call(functools.partial(gram_kernel, nz, bands), out_shape=(jax....]
  transfers between devices with their start and end apart: 2 -> 4, of which waited for: 2 -> 3; matrix products, arithmetic and copies ran while one was open for 0% -> 1% of each run, Pallas kernels for 0% -> 0%
where the time goes in v3:
time: 109 us; the launch traced here: 108 us
  blocking collectives  54.6 us (50%)
  Pallas kernels  32.4 us (30%)
  waiting for transfers between devices  12.7 us (12%)
  starting transfers between devices  5.55 us (5%)
  local copies, waits for them, and re-layouts  2.24 us (2%)
    pallas_call x3, Pallas kernels, call(): pl.pallas_call(kernel, out_shape=jax.ShapeDtypeStruct(shape, jnp.float32)...  25.8 us
    all_to_all x1, blocking collectives, transposed(): packed = lax.all_to_all(packed, area, 0, 0, tiled=True)  21.7 us
    all_to_all x1, blocking collectives, transposed(): filtered = lax.all_to_all(filtered, everyone, 0, 0, tiled=True)  16.8 us
    all_to_all x1, blocking collectives, transposed(): lax.all_to_all(partial.reshape(holders, rows // holders, LANES), same_cor...  16.1 us
    all_to_all x1, waiting for transfers between devices, transposed(): mine = lax.all_to_all(pieces, same_core, 0, 0, tiled=True)  8.7 us
    pallas_call x1, Pallas kernels, transposed(): pl.pallas_call(functools.partial(gram_kernel, nz, bands), out_shape=(jax....  4.35 us
    all_to_all x1, starting transfers between devices, transposed(): mine = lax.all_to_all(pieces, same_core, 0, 0, tiled=True)  3.67 us
    ppermute x1, waiting for transfers between devices, transposed(): other = lax.ppermute(own, 'band', swap)  2.87 us
  transfers between devices with their start and end apart: 4, of which 3 were waited for; matrix products, arithmetic and copies ran while one was open for 1% of the time, Pallas kernels for 0%

profile of v3, /device:TPU:0, one launch (start us, length us, event | category | flops | bytes accessed | tf_op | source)
XLA Modules:
  0.0 108.1 jit_solution(14666645244684735165)
XLA Ops:
  0.0 2.3 %shard_map.28 = f32[16,56,128]{2,1,0:T(8,128)} custom-call(f32[384,256]{1,0:T(8,128)} %bitcast.5, f32[6,8,8]{2,1,0:T(8,128)} %potential_ref.1), custom_call_target="tpu_custom_call" | custom-call | tf_op jit(solution)/shard_map/pallas_call | solution.py:334
  2.3 21.7 %all_to_all.20.in_ref = f32[16,56,128]{2,1,0:T(8,128)} all-to-all(f32[16,56,128]{2,1,0:T(8,128)} %shard_map.28), channel_id=1, replica_groups=mesh['chip'=2,'core'=2,'dy'=4,'band'=2] {'chip','core','dy'}, dimensions={0} | all-to-all | bytes 917504 | tf_op jit(solution)/shard_map/all_to_all | solution.py:344
  23.9 7.1 %shard_map.29 = f32[32,24,128]{2,1,0:T(8,128)} custom-call(f32[16,56,128]{2,1,0:T(8,128)} %all_to_all.20.in_ref), custom_call_target="tpu_custom_call" | custom-call | tf_op jit(solution)/shard_map/pallas_call | solution.py:311
  31.1 16.8 %all_to_all.21.own_ref = f32[32,24,128]{2,1,0:T(8,128)S(1)} all-to-all(f32[32,24,128]{2,1,0:T(8,128)} %shard_map.29), channel_id=1, replica_groups=mesh['chip'=2,'core'=2,'dy'=4,'band'=2] {'chip','core','dy','band'}, dimensions={0} | all-to-all | bytes 786432 | tf_op jit(solution)/shard_map/all_to_all | solution.py:356
  47.9 0.0 copy-start
  47.9 0.0 collective-permute-start
  47.9 0.6 pad_add_fusion.core_ref.place_ref
  48.5 1.1 %collective-permute-done.other_ref = f32[32,24,128]{2,1,0:T(8,128)S(1)} collective-permute-done((f32[32,24,128]{2,1,0:T(8,128)S(1)}, f32[32,24,128]{2,1,0:T(8,128)S(1)}, u32[]{:S(2)}, u32[]{:S(2)}) %collective-permute-start) | collective-permute-done | bytes 393248 | tf_op jit(solution)/shard_map/ppermute | solution.py:361
  49.6 0.0 copy-done
  49.6 0.0 copy-start.3
  49.6 0.7 copy-done.3
  50.4 4.3 %shard_map.30 = (f32[4,192,128]{2,1,0:T(8,128)}, f32[640,128]{1,0:T(8,128)}) custom-call(s32[2]{0:T(128)} %pad_add_fusion.core_ref.place_ref, f32[32,24,128]{2,1,0:T(8,128)} %copy-done, f32[32,24,128]{2,1,0:T(8,128)} %copy-done.3), custom_call_target="tpu_custom_call" | custom-call | tf_op jit(solution)/shard_map/pallas_call | solution.py:362
  54.7 16.1 %all_to_all.22.in_ref = f32[16,40,128]{2,1,0:T(8,128)} all-to-all(f32[16,40,128]{2,1,0:T(8,128)} %bitcast.6), channel_id=1, replica_groups=mesh['chip'=2,'core'=2,'dy'=4,'band'=2] {'chip','dy','band'}, dimensions={0} | all-to-all | bytes 655360 | tf_op jit(solution)/shard_map/all_to_all | solution.py:373
  70.8 1.7 %shard_map.31 = f32[16,40,128]{2,1,0:T(8,128)} custom-call(f32[16,40,128]{2,1,0:T(8,128)} %all_to_all.22.in_ref), custom_call_target="tpu_custom_call" | custom-call | tf_op jit(solution)/shard_map/pallas_call | solution.py:311
  72.5 0.0 copy-start.2
  72.5 3.7 %all-to-all-start.3 = ((f32[16,40,128]{2,1,0:T(8,128)}), f32[16,40,128]{2,1,0:T(8,128)S(1)}, u32[]{:S(2)}, u32[]{:S(2)}) async-start(f32[16,40,128]{2,1,0:T(8,128)} %shard_map.31), calls=%async_computation.3 | async-start | bytes 655360 | tf_op jit(solution)/shard_map/all_to_all | solution.py:375
  76.2 0.0 copy-done.2
  76.2 1.9 %collective-permute-start.2 = (f32[4,192,128]{2,1,0:T(8,128)S(1)}, f32[4,192,128]{2,1,0:T(8,128)S(1)}, u32[]{:S(2)}, u32[]{:S(2)}) collective-permute-start(f32[4,192,128]{2,1,0:T(8,128)S(1)} %copy-done.2), channel_id=1, source_target_pairs={{0,1},{1,0},{2,3},{3,2},{4,5},{5,4},{6,7},{7,6},{8,9},{9,8},{10,11... | collective-permute-start | bytes 1179656 | tf_op jit(solution)/shard_map/ppermute | solution.py:372
  78.1 8.7 %all-to-all-done.3.mine_ref = f32[16,40,128]{2,1,0:T(8,128)S(1)} async-done(((f32[16,40,128]{2,1,0:T(8,128)}), f32[16,40,128]{2,1,0:T(8,128)S(1)}, u32[]{:S(2)}, u32[]{:S(2)}) %all-to-all-start.3) | async-done | bytes 327712 | tf_op jit(solution)/shard_map/all_to_all | solution.py:375
  86.8 0.0 copy-start.1
  86.8 0.0 collective-permute-start.1
  86.8 2.9 %collective-permute-done.2.other_ref = f32[4,192,128]{2,1,0:T(8,128)S(1)} collective-permute-done((f32[4,192,128]{2,1,0:T(8,128)S(1)}, f32[4,192,128]{2,1,0:T(8,128)S(1)}, u32[]{:S(2)}, u32[]{:S(2)}) %collective-permute-start.2) | collective-permute-done | bytes 393248 | tf_op jit(solution)/shard_map/ppermute | solution.py:372
  89.7 0.0 copy-start.4
  89.7 0.0 collective-permute-done.1.theirs_ref
  89.7 0.0 copy-done.1
  89.7 0.7 copy-done.4
  90.4 0.0 copy-start.5
  90.4 0.7 copy-done.5
  91.2 16.9 %shard_map.32 = f32[384,256]{1,0:T(8,128)} custom-call(s32[2]{0:T(128)} %pad_add_fusion.core_ref.place_ref, f32[16,40,128]{2,1,0:T(8,128)} %copy-done.1, f32[16,40,128]{2,1,0:T(8,128)} %copy-done.5, f32[4,192,128]{2,1,0:T(8,128)} %get-tuple-element.8.own_ref, f32[4,192,128]{2,1,0:T(8,128)} %copy-done.4), custom_call_target="tpu_custom_call" | custom-call | tf_op jit(solution)/shard_map/pallas_call | solution.py:311
Async XLA Ops:
  47.9 1.7 %copy-start = (f32[32,24,128]{2,1,0:T(8,128)}, f32[32,24,128]{2,1,0:T(8,128)S(1)}, u32[]{:S(2)}) copy-start(f32[32,24,128]{2,1,0:T(8,128)S(1)} %all_to_all.21.own_ref) | copy-start | bytes 1179652
  47.9 1.7 %collective-permute-start = (f32[32,24,128]{2,1,0:T(8,128)S(1)}, f32[32,24,128]{2,1,0:T(8,128)S(1)}, u32[]{:S(2)}, u32[]{:S(2)}) collective-permute-start(f32[32,24,128]{2,1,0:T(8,128)S(1)} %all_to_all.21.own_ref), channel_id=1, source_target_pairs={{0,8},{8,0},{1,9},{9,1},{2,10},{10,2},{3,11},{11,3},{4,12},{12,4},... | collective-permute-start | bytes 1179656 | tf_op jit(solution)/shard_map/ppermute | solution.py:361
  49.6 0.7 copy-start.3
  72.5 3.7 %copy-start.2 = (f32[4,192,128]{2,1,0:T(8,128)S(1)}, f32[4,192,128]{2,1,0:T(8,128)}, u32[]{:S(2)}) copy-start(f32[4,192,128]{2,1,0:T(8,128)} %get-tuple-element.8.own_ref) | copy-start | bytes 1179652
  72.5 14.3 %all-to-all-start.3 = ((f32[16,40,128]{2,1,0:T(8,128)}), f32[16,40,128]{2,1,0:T(8,128)S(1)}, u32[]{:S(2)}, u32[]{:S(2)}) async-start(f32[16,40,128]{2,1,0:T(8,128)} %shard_map.31), calls=%async_computation.3 | async-start | bytes 655360 | tf_op jit(solution)/shard_map/all_to_all | solution.py:375
  76.2 13.4 %collective-permute-start.2 = (f32[4,192,128]{2,1,0:T(8,128)S(1)}, f32[4,192,128]{2,1,0:T(8,128)S(1)}, u32[]{:S(2)}, u32[]{:S(2)}) collective-permute-start(f32[4,192,128]{2,1,0:T(8,128)S(1)} %copy-done.2), channel_id=1, source_target_pairs={{0,1},{1,0},{2,3},{3,2},{4,5},{5,4},{6,7},{7,6},{8,9},{9,8},{10,11... | collective-permute-start | bytes 1179656 | tf_op jit(solution)/shard_map/ppermute | solution.py:372
  86.8 2.9 %copy-start.1 = (f32[16,40,128]{2,1,0:T(8,128)}, f32[16,40,128]{2,1,0:T(8,128)S(1)}, u32[]{:S(2)}) copy-start(f32[16,40,128]{2,1,0:T(8,128)S(1)} %all-to-all-done.3.mine_ref) | copy-start | bytes 983044
  86.8 2.9 %collective-permute-start.1 = (f32[16,40,128]{2,1,0:T(8,128)S(1)}, f32[16,40,128]{2,1,0:T(8,128)S(1)}, u32[]{:S(2)}, u32[]{:S(2)}) collective-permute-start(f32[16,40,128]{2,1,0:T(8,128)S(1)} %all-to-all-done.3.mine_ref), channel_id=1, source_target_pairs={{0,8},{8,0},{1,9},{9,1},{2,10},{10,2},{3,11},{11,3},{4,12},{12,4},... | collective-permute-start | bytes 983048 | tf_op jit(solution)/shard_map/ppermute | solution.py:376
  89.7 0.7 copy-start.4
  90.4 0.7 copy-start.5

commit v4 on v3

--- a/solution.py
+++ b/solution.py
@@ -6,6 +6,7 @@
 from jax.experimental import pallas as pl
 from jax.experimental.pallas import tpu as pltpu
 from jax.sharding import PartitionSpec as P
+
 
 DEGREE = 3
 LANES = 128
@@ -28,6 +29,8 @@
 centre_value = 7.0
 VMEM = pl.BlockSpec(memory_space=pltpu.VMEM)
 SMEM = pl.BlockSpec(memory_space=pltpu.SMEM)
+ANY = pl.BlockSpec(memory_space=pl.ANY)
+ROOM = pltpu.CompilerParams(vmem_limit_bytes=24 << 20)
 HIGHEST = lax.Precision.HIGHEST
 
 
@@ -137,16 +140,24 @@
     return upper_blocks(strips)[core :: CORES]
 
 
-def gram_kernel(nz, bands, core_ref, own_ref, other_ref, cells_ref, out_ref, paired):
+def gram_kernel(nz, bands, core_ref, own_in, other_in, cells_ref, out_ref, paired, own_ref, other_ref, arrived):
+    fetches = [
+        pltpu.make_async_copy(*copy, arrived.at[i])
+        for i, copy in enumerate(((own_in, own_ref), (other_in, other_ref)))
+    ]
+    for fetch in fetches:
+        fetch.start()
     columns = own_ref.shape[1]
     strips, rows, _ = cells_ref.shape
     per_band = strips // bands
-    for strip in range(strips):
-        first = nz * (strip % per_band)
-        for half, ref in enumerate((own_ref, other_ref)):
+    for half, ref in enumerate((own_ref, other_ref)):
+        fetches[half].wait()
+        for strip in range(strips):
+            first = nz * (strip % per_band)
             arrays = [ref[(first + g) * bands + strip // per_band] for g in range(nz)]
             for z, value in enumerate(swap_groups(arrays, LANES // nz)):
                 paired[strip, pl.ds(half * rows + z, columns, stride=nz), :] = value
+    for strip in range(strips):
         cells_ref[strip] = paired[strip, :rows, :]
     for core in range(CORES):
 
@@ -209,11 +220,11 @@
             pivots[tile] = jnp.where(sublane == row, pivot, pivots[tile])
             over = 1.0 / pivot
             factor = {t: column[k, t] * over for t in range(tile, tiles)}
-            factor[tile] = jnp.where(sublane > row, factor[tile], 0.0)
             for j in range(k + 1, first + PART):
                 value = spread_row(column[k, j // SUBLANES], j % SUBLANES)
                 for t in range(j // SUBLANES, tiles):
                     column[j, t] = column[j, t] - factor[t] * value
+            factor[tile] = jnp.where(sublane > row, factor[tile], 0.0)
             for c in range(strips):
                 value = spread_row(rows[tile][c], row)
                 for t in range(tile, tiles):
@@ -267,12 +278,20 @@
     lax.fori_loop(0, strips, step, 0)
 
 
-def finish_kernel(place_ref, mine_ref, theirs_ref, own_ref, other_ref, out_ref, matrix, inverse, work, done):
+def finish_kernel(place_ref, *refs):
+    inputs, out_ref, buffers, arrived = refs[:4], refs[4], refs[5:9], refs[9]
+    matrix, inverse, work, done = refs[10:]
+    fetches = [pltpu.make_async_copy(*copy, arrived.at[i]) for i, copy in enumerate(zip(inputs, buffers))]
+    for fetch in fetches:
+        fetch.start()
+    mine_ref, theirs_ref, own_ref, other_ref = buffers
     strips = own_ref.shape[0]
     cells = own_ref.shape[1]
     block = out_ref.shape[1]
     rows = mine_ref.shape[1]
     matrix[...] = jnp.zeros_like(matrix)
+    fetches[0].wait()
+    fetches[1].wait()
     for core in range(CORES):
 
         @pl.when(place_ref[0] == core)
@@ -285,6 +304,8 @@
                         matrix[top : top + SUBLANES, left : left + LANES] = ref[piece, row : row + SUBLANES, :]
 
     inverse_factor(matrix, inverse, work, done)
+    fetches[2].wait()
+    fetches[3].wait()
     band = place_ref[1]
     for b in range(strips * LANES // block):
 
@@ -314,6 +335,7 @@
         in_specs=specs,
         out_specs=VMEM,
         scratch_shapes=list(scratch),
+        compiler_params=ROOM,
     )(*args)
 
 
@@ -340,6 +362,7 @@
             pl.BlockSpec((size_x, size_y, nz), lambda i: (0, 0, 0)),
         ],
         out_specs=pl.BlockSpec((nz, columns + size_y, LANES), lambda i: (i, 0, 0)),
+        compiler_params=ROOM,
     )(states.reshape(cells, block), potential)
     packed = lax.all_to_all(packed, area, 0, 0, tiled=True)
     grid = (size_x * domains_x, size_y * domains_y, LANES)
@@ -365,26 +388,32 @@
             jax.ShapeDtypeStruct((strips, cells // bands, LANES), jnp.float32),
             jax.ShapeDtypeStruct((rows, LANES), jnp.float32),
         ),
-        in_specs=[SMEM, VMEM, VMEM],
+        in_specs=[SMEM, ANY, ANY],
         out_specs=(VMEM, VMEM),
-        scratch_shapes=[pltpu.VMEM((strips, CORES * cells // bands, LANES), jnp.float32)],
+        scratch_shapes=[
+            pltpu.VMEM((strips, CORES * cells // bands, LANES), jnp.float32),
+            pltpu.VMEM(filtered.shape, jnp.float32),
+            pltpu.VMEM(filtered.shape, jnp.float32),
+            pltpu.SemaphoreType.DMA((2,)),
+        ],
+        compiler_params=ROOM,
     )(place, filtered, neighbours)
     other = lax.ppermute(own, "band", swap)
     partial = lax.all_to_all(partial.reshape(holders, rows // holders, LANES), same_core, 0, 0, tiled=True)
     pieces = call(functools.partial(sum_kernel, float(cells * domains)), partial.shape, partial)
     mine = lax.all_to_all(pieces, same_core, 0, 0, tiled=True)
     theirs = lax.ppermute(mine, "core", swap)
-    result = call(
+    inputs = (mine, theirs, own, other)
+    result = pl.pallas_call(
         finish_kernel,
-        (cells, block),
-        place,
-        mine,
-        theirs,
-        own,
-        other,
-        scratch=[pltpu.VMEM((size, size), jnp.float32)] + factor_scratch(size),
-        scalars=1,
-    )
+        out_shape=jax.ShapeDtypeStruct((cells, block), jnp.float32),
+        in_specs=[SMEM] + [ANY] * len(inputs),
+        out_specs=VMEM,
+        scratch_shapes=[pltpu.VMEM(value.shape, jnp.float32) for value in inputs]
+        + [pltpu.SemaphoreType.DMA((len(inputs),)), pltpu.VMEM((size, size), jnp.float32)]
+        + factor_scratch(size),
+        compiler_params=ROOM,
+    )(place, *inputs)
     return result.reshape(states.shape)
 
 
@@ -419,7 +448,7 @@
 def haloed(states, potential):
     prev = states
     cur = (apply_ham(states, potential) - centre_value * states) / half_width
-    for step in range(1, DEGREE):
+    for _ in range(1, DEGREE):
         nxt = 2.0 * (apply_ham(cur, potential) - centre_value * cur) / half_width - prev
         prev, cur = (cur, nxt)
     block = cur.shape[3]
@@ -466,8 +495,9 @@
         else:
             body, over, x_axis = haloed, mesh, "dx"
         spec = P(x_axis, "dy", None, "band")
-        return jax.shard_map(
+        step = jax.shard_map(
             body, mesh=over, in_specs=(spec, P(x_axis, "dy", None)), out_specs=spec, check_vma=False
-        )(states, potential)
+        )
+        return step(states, potential)
 
     return run

time: 109 us -> 100 us (0.917)
  Pallas kernels: 32.4 us -> 26.6 us
  blocking collectives: 54.6 us -> 52.8 us
    pallas_call x3 -> x2, Pallas kernels: 25.8 us -> 6.13 us  [call(): pl.pallas_call(kernel, out_shape=jax.ShapeDtypeStruct(shape, jnp.float32)...]
    pallas_call x0 -> x1, Pallas kernels: none -> 16.6 us  [transposed(): pl.pallas_call(finish_kernel, out_shape=jax.ShapeDtypeStruct((cells, bloc...]
    pallas_call x1, Pallas kernels: 2.26 us -> 0.72 us  [transposed(): pl.pallas_call(functools.partial(pack_kernel, nz), out_shape=jax.ShapeDty...]
    all_to_all x1, blocking collectives: 16.1 us -> 14.8 us  [transposed(): lax.all_to_all(partial.reshape(holders, rows // holders, LANES), same_cor...]
    pallas_call x1, Pallas kernels: 4.35 us -> 3.18 us  [transposed(): pl.pallas_call(functools.partial(gram_kernel, nz, bands), out_shape=(jax....]
    unnamed x12 -> x4, local copies, waits for them, and re-layouts: 2.24 us -> 1.73 us
  transfers between devices with their start and end apart: 4 -> 4, of which waited for: 3 -> 3; matrix products, arithmetic and copies ran while one was open for 1% -> 0% of each run, Pallas kernels for 0% -> 0%
where the time goes in v4:
time: 100 us; the launch traced here: 99.9 us
  blocking collectives  52.8 us (53%)
  Pallas kernels  26.6 us (27%)
  waiting for transfers between devices  13.3 us (13%)
  starting transfers between devices  5.35 us (5%)
  local copies, waits for them, and re-layouts  1.73 us (2%)
    all_to_all x1, blocking collectives, transposed(): packed = lax.all_to_all(packed, area, 0, 0, tiled=True)  21.4 us
    all_to_all x1, blocking collectives, transposed(): filtered = lax.all_to_all(filtered, everyone, 0, 0, tiled=True)  16.6 us
    pallas_call x1, Pallas kernels, transposed(): pl.pallas_call(finish_kernel, out_shape=jax.ShapeDtypeStruct((cells, bloc...  16.6 us
    all_to_all x1, blocking collectives, transposed(): lax.all_to_all(partial.reshape(holders, rows // holders, LANES), same_cor...  14.8 us
    all_to_all x1, waiting for transfers between devices, transposed(): mine = lax.all_to_all(pieces, same_core, 0, 0, tiled=True)  8.77 us
    pallas_call x2, Pallas kernels, call(): pl.pallas_call(kernel, out_shape=jax.ShapeDtypeStruct(shape, jnp.float32)...  6.13 us
    all_to_all x1, starting transfers between devices, transposed(): mine = lax.all_to_all(pieces, same_core, 0, 0, tiled=True)  3.54 us
    pallas_call x1, Pallas kernels, transposed(): pl.pallas_call(functools.partial(gram_kernel, nz, bands), out_shape=(jax....  3.18 us
  transfers between devices with their start and end apart: 4, of which 3 were waited for; matrix products, arithmetic and copies ran while one was open for 0% of the time, Pallas kernels for 0%

profile of v4, /device:TPU:0, one launch (start us, length us, event | category | flops | bytes accessed | tf_op | source)
XLA Modules:
  0.0 99.9 jit_solution(14659792610087599430)
XLA Ops:
  0.0 0.0 copy-start
  0.0 1.0 copy-done
  1.0 0.0 copy-start.1
  1.0 0.7 copy-done.1
  1.7 0.7 shard_map.28
  2.5 21.4 %all_to_all.20.in_ref = f32[16,56,128]{2,1,0:T(8,128)S(1)} all-to-all(f32[16,56,128]{2,1,0:T(8,128)S(1)} %shard_map.28), channel_id=1, replica_groups=mesh['chip'=2,'core'=2,'dy'=4,'band'=2] {'chip','core','dy'}, dimensions={0} | all-to-all | bytes 917504 | tf_op jit(solution)/shard_map/all_to_all | solution.py:367
  23.8 5.4 %shard_map.29 = f32[32,24,128]{2,1,0:T(8,128)S(1)} custom-call(f32[16,56,128]{2,1,0:T(8,128)S(1)} %all_to_all.20.in_ref), custom_call_target="tpu_custom_call" | custom-call | tf_op jit(solution)/shard_map/pallas_call | solution.py:332
  29.2 16.6 %all_to_all.21.own_in = f32[32,24,128]{2,1,0:T(8,128)S(1)} all-to-all(f32[32,24,128]{2,1,0:T(8,128)S(1)} %shard_map.29), channel_id=1, replica_groups=mesh['chip'=2,'core'=2,'dy'=4,'band'=2] {'chip','core','dy','band'}, dimensions={0} | all-to-all | bytes 786432 | tf_op jit(solution)/shard_map/all_to_all | solution.py:379
  45.8 0.0 collective-permute-start
  45.8 0.1 pad_add_fusion.core_ref.place_ref
  45.9 1.6 %collective-permute-done.other_in = f32[32,24,128]{2,1,0:T(8,128)S(1)} collective-permute-done((f32[32,24,128]{2,1,0:T(8,128)S(1)}, f32[32,24,128]{2,1,0:T(8,128)S(1)}, u32[]{:S(2)}, u32[]{:S(2)}) %collective-permute-start) | collective-permute-done | bytes 393248 | tf_op jit(solution)/shard_map/ppermute | solution.py:384
  47.5 3.2 %shard_map.30 = (f32[4,192,128]{2,1,0:T(8,128)S(1)}, f32[640,128]{1,0:T(8,128)S(1)}) custom-call(s32[2]{0:T(128)S(1)} %pad_add_fusion.core_ref.place_ref, f32[32,24,128]{2,1,0:T(8,128)S(1)} %all_to_all.21.own_in, f32[32,24,128]{2,1,0:T(8,128)S(1)} %collective-permute-done.other_in), custom_call_target="tpu_custom_call" | custom-call | tf_op jit(solution)/shard_map/pallas_call | solution.py:385
  50.7 14.8 %all_to_all.22.in_ref = f32[16,40,128]{2,1,0:T(8,128)S(1)} all-to-all(f32[16,40,128]{2,1,0:T(8,128)S(1)} %bitcast.6), channel_id=1, replica_groups=mesh['chip'=2,'core'=2,'dy'=4,'band'=2] {'chip','dy','band'}, dimensions={0} | all-to-all | bytes 655360 | tf_op jit(solution)/shard_map/all_to_all | solution.py:402
  65.5 0.8 shard_map.31
  66.3 3.5 %all-to-all-start.3 = ((f32[16,40,128]{2,1,0:T(8,128)}), f32[16,40,128]{2,1,0:T(8,128)S(1)}, u32[]{:S(2)}, u32[]{:S(2)}) async-start(f32[16,40,128]{2,1,0:T(8,128)} %shard_map.31), calls=%async_computation.3 | async-start | bytes 655360 | tf_op jit(solution)/shard_map/all_to_all | solution.py:404
  69.8 1.8 %collective-permute-start.2 = (f32[4,192,128]{2,1,0:T(8,128)S(1)}, f32[4,192,128]{2,1,0:T(8,128)S(1)}, u32[]{:S(2)}, u32[]{:S(2)}) collective-permute-start(f32[4,192,128]{2,1,0:T(8,128)S(1)} %get-tuple-element.8.refs_2_), channel_id=1, source_target_pairs={{0,1},{1,0},{2,3},{3,2},{4,5},{5,4},{6,7},{7,6},{8,9},{9,8},{10,11... | collective-permute-start | bytes 1179656 | tf_op jit(solution)/shard_map/ppermute | solution.py:401
  71.6 8.8 %all-to-all-done.3.refs_0_ = f32[16,40,128]{2,1,0:T(8,128)S(1)} async-done(((f32[16,40,128]{2,1,0:T(8,128)}), f32[16,40,128]{2,1,0:T(8,128)S(1)}, u32[]{:S(2)}, u32[]{:S(2)}) %all-to-all-start.3) | async-done | bytes 327712 | tf_op jit(solution)/shard_map/all_to_all | solution.py:404
  80.4 0.0 collective-permute-start.1
  80.4 2.9 %collective-permute-done.2.refs_3_ = f32[4,192,128]{2,1,0:T(8,128)S(1)} collective-permute-done((f32[4,192,128]{2,1,0:T(8,128)S(1)}, f32[4,192,128]{2,1,0:T(8,128)S(1)}, u32[]{:S(2)}, u32[]{:S(2)}) %collective-permute-start.2) | collective-permute-done | bytes 393248 | tf_op jit(solution)/shard_map/ppermute | solution.py:401
  83.3 0.0 collective-permute-done.1.refs_1_
  83.3 16.6 %shard_map.32 = f32[384,256]{1,0:T(8,128)} custom-call(s32[2]{0:T(128)S(1)} %pad_add_fusion.core_ref.place_ref, f32[16,40,128]{2,1,0:T(8,128)S(1)} %all-to-all-done.3.refs_0_, f32[16,40,128]{2,1,0:T(8,128)S(1)} %collective-permute-done.1.refs_1_, f32[4,192,128]{2,1,0:T(8,128)S(1)} %get-tuple-element.8.refs_2_, f32[4,192,128]{2,1,0:T(8,128)S(1)} %collective-permute-done.2.refs_3_), custom_call_target="tpu_custom_call" | custom-call | tf_op jit(solution)/shard_map/pallas_call | solution.py:407
Async XLA Ops:
  0.0 1.0 copy-start
  1.0 0.7 copy-start.1
  45.8 1.7 %collective-permute-start = (f32[32,24,128]{2,1,0:T(8,128)S(1)}, f32[32,24,128]{2,1,0:T(8,128)S(1)}, u32[]{:S(2)}, u32[]{:S(2)}) collective-permute-start(f32[32,24,128]{2,1,0:T(8,128)S(1)} %all_to_all.21.own_in), channel_id=1, source_target_pairs={{0,8},{8,0},{1,9},{9,1},{2,10},{10,2},{3,11},{11,3},{4,12},{12,4},... | collective-permute-start | bytes 1179656 | tf_op jit(solution)/shard_map/ppermute | solution.py:384
  66.3 14.1 %all-to-all-start.3 = ((f32[16,40,128]{2,1,0:T(8,128)}), f32[16,40,128]{2,1,0:T(8,128)S(1)}, u32[]{:S(2)}, u32[]{:S(2)}) async-start(f32[16,40,128]{2,1,0:T(8,128)} %shard_map.31), calls=%async_computation.3 | async-start | bytes 655360 | tf_op jit(solution)/shard_map/all_to_all | solution.py:404
  69.8 13.4 %collective-permute-start.2 = (f32[4,192,128]{2,1,0:T(8,128)S(1)}, f32[4,192,128]{2,1,0:T(8,128)S(1)}, u32[]{:S(2)}, u32[]{:S(2)}) collective-permute-start(f32[4,192,128]{2,1,0:T(8,128)S(1)} %get-tuple-element.8.refs_2_), channel_id=1, source_target_pairs={{0,1},{1,0},{2,3},{3,2},{4,5},{5,4},{6,7},{7,6},{8,9},{9,8},{10,11... | collective-permute-start | bytes 1179656 | tf_op jit(solution)/shard_map/ppermute | solution.py:401
  80.4 2.9 %collective-permute-start.1 = (f32[16,40,128]{2,1,0:T(8,128)S(1)}, f32[16,40,128]{2,1,0:T(8,128)S(1)}, u32[]{:S(2)}, u32[]{:S(2)}) collective-permute-start(f32[16,40,128]{2,1,0:T(8,128)S(1)} %all-to-all-done.3.refs_0_), channel_id=1, source_target_pairs={{0,8},{8,0},{1,9},{9,1},{2,10},{10,2},{3,11},{11,3},{4,12},{12,4},... | collective-permute-start | bytes 983048 | tf_op jit(solution)/shard_map/ppermute | solution.py:405

commit v5 on v3

v5 whole, which is shorter than its diff:
```python
import functools

import jax
import jax.numpy as jnp
from jax import lax
from jax.experimental import pallas as pl
from jax.experimental.pallas import tpu as pltpu
from jax.sharding import PartitionSpec as P


DEGREE = 3
LANES = 128
SUBLANES = 8
PANEL = 32
PART = 16
CORES = 2
PRODUCTS = 6

coeffs = (
    -5369.0 / 1800.0,
    12.0 / 7.0,
    -15.0 / 56.0,
    10.0 / 189.0,
    -1.0 / 112.0,
    2.0 / 1925.0,
    -1.0 / 16632.0,
)
WIDTH = len(coeffs) - 1
half_width = 5.0
centre_value = 7.0
VMEM = pl.BlockSpec(memory_space=pltpu.VMEM)
SMEM = pl.BlockSpec(memory_space=pltpu.SMEM)
HBM = pl.BlockSpec(memory_space=pltpu.HBM)
ROOM = pltpu.CompilerParams(vmem_limit_bytes=24 << 20)
HIGHEST = lax.Precision.HIGHEST


def dot(a, b, dims):
    return lax.dot_general(a, b, (dims, ((), ())), precision=HIGHEST, preferred_element_type=jnp.float32)


def split(value):
    high = value.astype(jnp.bfloat16)
    rest = value - high.astype(jnp.float32)
    middle = rest.astype(jnp.bfloat16)
    return high, middle, (rest - middle.astype(jnp.float32)).astype(jnp.bfloat16)


def left_parts(parts):
    high, middle, low = parts
    return [high, high, middle, middle, high, low]


def right_parts(parts):
    high, middle, low = parts
    return [high, middle, high, middle, low, high]


def outer(left, right):
    left = jnp.concatenate(left_parts(left), axis=0)
    right = jnp.concatenate(right_parts(right), axis=0)
    return lax.dot_general(left, right, (((0,), (0,)), ((), ())), preferred_element_type=jnp.float32)


def product(left, right):
    left = jnp.concatenate(left_parts(left), axis=1)
    right = jnp.concatenate(right_parts(right), axis=0)
    return lax.dot_general(left, right, (((1,), (0,)), ((), ())), preferred_element_type=jnp.float32)


def swap_groups(arrays, group):
    count = len(arrays)
    lane = lax.broadcasted_iota(jnp.int32, arrays[0].shape, 1)
    bit = 1
    while bit < count:
        upper = (lane // (group * bit)) % 2 == 1
        out = list(arrays)
        for i in range(count):
            if i & bit == 0:
                low, high = arrays[i], arrays[i | bit]
                out[i] = jnp.where(upper, pltpu.roll(high, group * bit, 1), low)
                out[i | bit] = jnp.where(upper, high, pltpu.roll(low, LANES - group * bit, 1))
        arrays = out
        bit *= 2
    return arrays


def pack_kernel(nz, states_in, potential_in, out_ref, states, potential, arrived):
    halves = range(states.shape[0])
    fetches = [
        pltpu.make_async_copy(states_in.at[:, pl.ds(LANES * half, LANES)], states.at[half], arrived.at[half])
        for half in halves
    ]
    last = pltpu.make_async_copy(potential_in, potential, arrived.at[len(fetches)])
    for fetch in [last] + fetches:
        fetch.start()
    columns = states.shape[1] // nz
    row = lax.broadcasted_iota(jnp.int32, (nz, LANES), 0)
    lane = lax.broadcasted_iota(jnp.int32, (nz, LANES), 1)
    last.wait()
    packed = jnp.zeros((potential.shape[1], LANES), jnp.float32)
    for x in range(potential.shape[0]):
        spread = jnp.where(lane == row + nz * x, 1.0, 0.0)
        packed = packed + dot(potential[x], spread, ((1,), (0,)))
    for i in range(out_ref.shape[0]):
        out_ref[i, columns:, :] = packed
    for half in halves:
        fetches[half].wait()
        arrays = [states[half, pl.ds(z, columns, stride=nz), :] for z in range(nz)]
        for g, value in enumerate(swap_groups(arrays, LANES // nz)):
            out_ref[half * nz + g, :columns, :] = value


def filter_kernel(nz, domains_y, size_x, size_y, in_ref, out_ref, field, potential):
    domains = in_ref.shape[0]
    total_x = size_x * (domains // domains_y)
    total_y = size_y * domains_y
    columns = size_x * size_y
    group = LANES // nz
    shares = out_ref.shape[0] // domains
    share = size_x // shares

    def place(i, x):
        return size_x * (i // domains_y) + x, size_y * (i % domains_y)

    def keep(which, x, rows, value):
        field[which, WIDTH + x, rows, :] = value
        if x < WIDTH:
            field[which, WIDTH + total_x + x, rows, :] = value
        if x >= total_x - WIDTH:
            field[which, WIDTH + x - total_x, rows, :] = value

    packed = in_ref[:, columns:, :].reshape(domains * size_y, LANES)
    source = lax.broadcasted_iota(jnp.int32, (LANES, LANES), 0)
    target = lax.broadcasted_iota(jnp.int32, (LANES, LANES), 1)
    for x in range(size_x):
        spread = jnp.where(source == nz * x + target // group, 1.0, 0.0)
        values = dot(packed, spread, ((1,), (0,)))
        for i in range(domains):
            at_x, at_y = place(i, x)
            rows = slice(at_y, at_y + size_y)
            potential[at_x, rows, :] = values[size_y * i : size_y * (i + 1)] - centre_value
            keep(0, at_x, rows, in_ref[i, size_y * x : size_y * (x + 1), :])

    def ring(distance, size):
        value = jnp.zeros(distance.shape, jnp.float32)
        for k in range(1, WIDTH + 1):
            for shift in (k, -k):
                value = value + jnp.where(distance == shift % size, coeffs[k], 0.0)
        return value

    along_z = ring((source // group - target // group + nz) % nz, nz)
    along_z = jnp.where((source - target) % group == 0, along_z, 0.0)
    along_z = along_z + jnp.where(source == target, 3.0 * coeffs[0], 0.0)
    along_z = jnp.concatenate(right_parts(split(along_z)), axis=0)
    shape = (total_y, PRODUCTS * total_y)
    row = lax.broadcasted_iota(jnp.int32, shape, 0)
    lane = lax.broadcasted_iota(jnp.int32, shape, 1)
    ring_y = ring((row - lane % total_y + total_y) % total_y, total_y)
    along_y = jnp.zeros(shape, jnp.float32)
    for part, value in enumerate(left_parts(split(ring_y))):
        along_y = jnp.where(lane // total_y == part, value.astype(jnp.float32), along_y)
    along_y = along_y.astype(jnp.bfloat16)

    for step in range(DEGREE):
        now, other = step % 2, (step + 1) % 2
        scale = 1.0 / half_width if step == 0 else 2.0 / half_width
        for x in range(total_x):
            value = field[now, WIDTH + x]
            parts = split(value)
            lap = lax.dot_general(
                jnp.concatenate(left_parts(parts), axis=1),
                along_z,
                (((1,), (0,)), ((), ())),
                preferred_element_type=jnp.float32,
            )
            lap = lap + lax.dot_general(
                along_y,
                jnp.concatenate(right_parts(parts), axis=0),
                (((1,), (0,)), ((), ())),
                preferred_element_type=jnp.float32,
            )
            for k in range(1, WIDTH + 1):
                lap = lap + coeffs[k] * (field[now, WIDTH + x + k] + field[now, WIDTH + x - k])
            result = (potential[x] * value - 0.5 * lap) * scale
            if step > 0:
                result = result - field[other, WIDTH + x]
            if step + 1 < DEGREE:
                keep(other, x, slice(None), result)
                continue
            for j in range(domains_y):
                i = x // size_x * domains_y + j
                row = size_y * (x % share)
                out_ref[i * shares + x % size_x // share, row : row + size_y, :] = result[size_y * j : size_y * (j + 1)]


def unpack(nz, in_ref, bands, strip, out_ref, offset):
    per_band = nz_strips(in_ref, nz, bands)
    first = nz * (strip % per_band)
    arrays = [in_ref[(first + g) * bands + strip // per_band] for g in range(nz)]
    for z, value in enumerate(swap_groups(arrays, LANES // nz)):
        out_ref[strip, pl.ds(offset + z, in_ref.shape[1], stride=nz), :] = value


def nz_strips(in_ref, nz, bands):
    return in_ref.shape[0] // (nz * bands)


def upper_blocks(strips):
    return [(i, j) for i in range(strips) for j in range(i, strips)]


def share_of(strips, core):
    return upper_blocks(strips)[core :: CORES]


def gram_kernel(nz, bands, core_ref, own_ref, other_ref, cells_ref, out_ref, paired):
    strips, rows, _ = cells_ref.shape
    for strip in range(strips):
        unpack(nz, own_ref, bands, strip, paired, 0)
        unpack(nz, other_ref, bands, strip, paired, rows)
        cells_ref[strip] = paired[strip, :rows, :]
    parts = [split(paired[strip]) for strip in range(strips)]
    for core in range(CORES):

        @pl.when(core_ref[0] == core)
        def _(core=core):
            for at, (i, j) in enumerate(share_of(strips, core)):
                out_ref[LANES * at : LANES * (at + 1), :] = outer(parts[i], parts[j])


def sum_kernel(total, in_ref, out_ref):
    value = in_ref[0]
    for i in range(1, in_ref.shape[0]):
        value = value + in_ref[i]
    value = value / total
    for i in range(out_ref.shape[0]):
        out_ref[i] = value


def spread_row(value, row):
    return jnp.broadcast_to(value[row : row + 1, :], value.shape)


def eliminate(rows, start):
    rows = list(rows)
    tiles = len(rows)
    sublane = lax.broadcasted_iota(jnp.int32, (SUBLANES, LANES), 0)
    at = lax.broadcasted_iota(jnp.int32, (SUBLANES, LANES), 1) - start
    pivots = [jnp.ones((SUBLANES, LANES), jnp.float32) for _ in range(tiles)]
    for first in range(0, PANEL, PART):
        column = {
            (j, t): jnp.broadcast_to(rows[t][:, start + j : start + j + 1], (SUBLANES, LANES))
            for j in range(first, first + PART)
            for t in range(j // SUBLANES, tiles)
        }
        inside = (at >= first) & (at < first + PART)
        for t in range(tiles):
            rows[t] = jnp.where(inside, jnp.where(at == sublane + SUBLANES * t, 1.0, 0.0), rows[t])
        for k in range(first, first + PART):
            tile, row = k // SUBLANES, k % SUBLANES
            pivot = spread_row(column[k, tile], row)
            pivots[tile] = jnp.where(sublane == row, pivot, pivots[tile])
            over = 1.0 / pivot
            factor = {t: column[k, t] * over for t in range(tile, tiles)}
            for j in range(k + 1, first + PART):
                value = spread_row(column[k, j // SUBLANES], j % SUBLANES)
                for t in range(j // SUBLANES, tiles):
                    column[j, t] = column[j, t] - factor[t] * value
            factor[tile] = jnp.where(sublane > row, factor[tile], 0.0)
            value = spread_row(rows[tile], row)
            for t in range(tile, tiles):
                rows[t] = rows[t] - factor[t] * value
    return [rows[t] * lax.rsqrt(pivots[t]) for t in range(tiles)]


def inverse_of_block(value):
    rest = [value[t : t + SUBLANES] for t in range(0, LANES, SUBLANES)]
    lane = lax.broadcasted_iota(jnp.int32, (SUBLANES, LANES), 1)
    out = []
    for start in range(0, LANES, PANEL):
        end = start + PANEL
        rows = eliminate(rest[start // SUBLANES : end // SUBLANES], start)
        out += [jnp.where(lane < end, row, 0.0) for row in rows]
        if end < LANES:
            parts = split(jnp.concatenate(rows, axis=0))
            update = outer(parts, parts)
            for t in range(end // SUBLANES, LANES // SUBLANES):
                old = jnp.where((lane >= start) & (lane < end), 0.0, rest[t])
                rest[t] = old - update[SUBLANES * t : SUBLANES * (t + 1)]
    return jnp.concatenate(out, axis=0)


def beside(left, right):
    return tuple(jnp.concatenate(pair, axis=1) for pair in zip(left, right))


def inverse_factor(matrix, inverse):
    size = matrix.shape[0]
    for low in range(0, size, LANES):
        high = low + LANES
        rows = slice(low, high)
        block = inverse_of_block(matrix[rows, rows])
        left = split(block)
        inverse[rows, rows] = block
        if high < size:
            inverse[rows, high:] = jnp.zeros((LANES, size - high), jnp.float32)
            following = slice(high, high + LANES)
            above = split(product(left, split(matrix[rows, following])))
            matrix[following, following] = matrix[following, following] - outer(above, above)
            if high + LANES < size:
                above = beside(above, split(product(left, split(matrix[rows, high + LANES :]))))
        below = left
        if low:
            value = product(left, split(matrix[rows, :low]))
            inverse[rows, :low] = value
            below = beside(split(value), left)
        for at in range(high, size, LANES):
            mine = tuple(part[:, at - high : at - high + LANES] for part in above)
            target = slice(at, at + LANES)
            update = outer(mine, below)
            if low:
                matrix[target, :low] = matrix[target, :low] - update[:, :low]
            matrix[target, rows] = -update[:, low:]
            first = max(at, high + LANES)
            if first < size:
                update = outer(mine, tuple(part[:, first - high :] for part in above))
                matrix[target, first:] = matrix[target, first:] - update


def finish_kernel(place_ref, mine_ref, theirs_ref, own_ref, other_ref, out_ref, matrix, inverse):
    strips = own_ref.shape[0]
    cells = own_ref.shape[1]
    block = out_ref.shape[1]
    rows = mine_ref.shape[1]
    for core in range(CORES):

        @pl.when(place_ref[0] == core)
        def _(core=core):
            for ref, holder in ((mine_ref, core), (theirs_ref, 1 - core)):
                for at, (i, j) in enumerate(share_of(strips, holder)):
                    for r in range(0, LANES, SUBLANES):
                        piece, row = divmod(LANES * at + r, rows)
                        top, left = LANES * i + r, LANES * j
                        matrix[top : top + SUBLANES, left : left + LANES] = ref[piece, row : row + SUBLANES, :]

    inverse_factor(matrix, inverse)
    band = place_ref[1]
    for b in range(strips * LANES // block):

        @pl.when(band == b)
        def _(b=b):
            used = block * (b + 1)
            mine = inverse[block * b : used, :used]
            for share, ref in ((b, own_ref), (1 - b, other_ref)):
                value = jnp.concatenate([ref[s] for s in range(used // LANES)], axis=1)
                out_ref[cells * share : cells * (share + 1), :] = dot(value, mine, ((1,), (1,)))


def factor_kernel(in_ref, out_ref, matrix):
    matrix[...] = in_ref[...]
    inverse_factor(matrix, out_ref)


def call(kernel, shape, *args, scratch=(), scalars=0):
    specs = [SMEM] * scalars + [VMEM] * (len(args) - scalars)
    return pl.pallas_call(
        kernel,
        out_shape=jax.ShapeDtypeStruct(shape, jnp.float32),
        in_specs=specs,
        out_specs=VMEM,
        scratch_shapes=list(scratch),
        compiler_params=ROOM,
    )(*args)


def transposed(states, potential):
    size_x, size_y, nz, block = states.shape
    domains_y = lax.axis_size("dy")
    domains_x = lax.axis_size("chip") * CORES
    domains = domains_x * domains_y
    bands = lax.axis_size("band")
    cells = size_x * size_y * nz
    columns = size_x * size_y
    area = ("chip", "core", "dy")
    everyone = area + ("band",)
    same_core = ("chip", "dy", "band")
    swap = [(0, 1), (1, 0)]
    place = jnp.stack([lax.axis_index("core"), lax.axis_index("band")]).astype(jnp.int32)

    packed = pl.pallas_call(
        functools.partial(pack_kernel, nz),
        out_shape=jax.ShapeDtypeStruct((domains, columns + size_y, LANES), jnp.float32),
        in_specs=[HBM, HBM],
        out_specs=VMEM,
        scratch_shapes=[
            pltpu.VMEM((block // LANES, cells, LANES), jnp.float32),
            pltpu.VMEM(potential.shape, jnp.float32),
            pltpu.SemaphoreType.DMA((block // LANES + 1,)),
        ],
        compiler_params=ROOM,
    )(*(pltpu.with_memory_space_constraint(v, pltpu.HBM) for v in (states.reshape(cells, block), potential)))
    packed = lax.all_to_all(packed, area, 0, 0, tiled=True)
    grid = (size_x * domains_x, size_y * domains_y, LANES)
    filtered = call(
        functools.partial(filter_kernel, nz, domains_y, size_x, size_y),
        (domains * bands, columns // bands, LANES),
        packed,
        scratch=[
            pltpu.VMEM((2, grid[0] + 2 * WIDTH) + grid[1:], jnp.float32),
            pltpu.VMEM(grid, jnp.float32),
        ],
    )
    filtered = lax.all_to_all(filtered, everyone, 0, 0, tiled=True)
    size = block * bands
    strips = size // LANES
    rows = len(share_of(strips, 0)) * LANES
    holders = domains * bands // CORES
    neighbours = lax.ppermute(filtered, "core", swap)
    own, partial = pl.pallas_call(
        functools.partial(gram_kernel, nz, bands),
        out_shape=(
            jax.ShapeDtypeStruct((strips, cells // bands, LANES), jnp.float32),
            jax.ShapeDtypeStruct((rows, LANES), jnp.float32),
        ),
        in_specs=[SMEM, VMEM, VMEM],
        out_specs=(VMEM, VMEM),
        scratch_shapes=[pltpu.VMEM((strips, CORES * cells // bands, LANES), jnp.float32)],
        compiler_params=ROOM,
    )(place, filtered, neighbours)
    other = lax.ppermute(own, "band", swap)
    partial = lax.all_to_all(partial.reshape(holders, rows // holders, LANES), same_core, 0, 0, tiled=True)
    pieces = call(functools.partial(sum_kernel, float(cells * domains)), partial.shape, partial)
    mine = lax.all_to_all(pieces, same_core, 0, 0, tiled=True)
    theirs = lax.ppermute(mine, "core", swap)
    result = call(
        finish_kernel,
        (cells, block),
        place,
        mine,
        theirs,
        own,
        other,
        scratch=[pltpu.VMEM((size, size), jnp.float32)] * 2,
        scalars=1,
    )
    return result.reshape(states.shape)


def with_halo(cells, axis, dim, width):
    count = lax.axis_size(axis)
    size = cells.shape[dim]
    head = lax.slice_in_dim(cells, 0, width, axis=dim)
    tail = lax.slice_in_dim(cells, size - width, size, axis=dim)
    before = lax.ppermute(tail, axis, [(i, (i + 1) % count) for i in range(count)])
    after = lax.ppermute(head, axis, [((i + 1) % count, i) for i in range(count)])
    return jnp.concatenate([before, cells, after], axis=dim)


def apply_ham(field, potential):
    padded_x = with_halo(field, "dx", 0, WIDTH)
    padded_y = with_halo(field, "dy", 1, WIDTH)
    size_x = field.shape[0]
    size_y = field.shape[1]
    lap = 3.0 * coeffs[0] * field
    for shift in range(1, WIDTH + 1):
        near = (
            padded_x[WIDTH + shift : WIDTH + shift + size_x]
            + padded_x[WIDTH - shift : WIDTH - shift + size_x]
            + padded_y[:, WIDTH + shift : WIDTH + shift + size_y]
            + padded_y[:, WIDTH - shift : WIDTH - shift + size_y]
        )
        near = near + jnp.roll(field, shift, 2) + jnp.roll(field, -shift, 2)
        lap = lap + coeffs[shift] * near
    return -0.5 * lap + potential[..., None] * field


def haloed(states, potential):
    prev = states
    cur = (apply_ham(states, potential) - centre_value * states) / half_width
    for _ in range(1, DEGREE):
        nxt = 2.0 * (apply_ham(cur, potential) - centre_value * cur) / half_width - prev
        prev, cur = (cur, nxt)
    block = cur.shape[3]
    cells = cur.shape[0] * cur.shape[1] * cur.shape[2]
    local = cur.reshape(cells, block)
    gathered = lax.all_gather(local, "band", axis=1, tiled=True)
    total = cells * lax.axis_size("dx") * lax.axis_size("dy")
    partial = jnp.dot(gathered.T, gathered, precision=HIGHEST, preferred_element_type=jnp.float32) / total
    correlation = lax.psum(partial, ("dx", "dy"))
    size = correlation.shape[0]
    if size % LANES == 0:
        inverse = call(factor_kernel, (size, size), correlation, scratch=[pltpu.VMEM((size, size), jnp.float32)])
    else:
        factor = jnp.linalg.cholesky(correlation)
        inverse = jax.scipy.linalg.solve_triangular(factor, jnp.eye(size, dtype=jnp.float32), lower=True)
    my_rows = lax.dynamic_slice_in_dim(inverse, lax.axis_index("band") * block, block, 0)
    result = jnp.dot(gathered, my_rows.T, precision=HIGHEST, preferred_element_type=jnp.float32)
    return result.reshape(cur.shape)


def solution(mesh):
    domains_x, domains_y, bands = (mesh.shape[name] for name in ("dx", "dy", "band"))
    domains = domains_x * domains_y

    def run(states, potential):
        total_x, total_y, nz, size = states.shape
        size_x, size_y, block = total_x // domains_x, total_y // domains_y, size // bands
        if (
            nz == SUBLANES
            and size_y == SUBLANES
            and nz * size_x <= LANES
            and block * nz == LANES * domains
            and block % LANES == 0
            and bands == 2
            and size_x % bands == 0
            and domains_x % CORES == 0
            and (size // LANES) * (size // LANES + 1) * LANES % (2 * domains * bands * SUBLANES) == 0
            and total_x > 2 * WIDTH
            and total_y > 2 * WIDTH
        ):
            devices = mesh.devices.reshape(domains_x // CORES, CORES, domains_y, bands)
            body, over = transposed, jax.sharding.Mesh(devices, ("chip", "core", "dy", "band"))
            x_axis = ("chip", "core")
        else:
            body, over, x_axis = haloed, mesh, "dx"
        spec = P(x_axis, "dy", None, "band")
        step = jax.shard_map(
            body, mesh=over, in_specs=(spec, P(x_axis, "dy", None)), out_specs=spec, check_vma=False
        )
        return step(states, potential)

    return run
```

time: 109 us -> 95.6 us (0.88)
  Pallas kernels: 32.4 us -> 23.8 us
  local copies, waits for them, and re-layouts: 2.24 us -> 0 us
  blocking collectives: 54.6 us -> 52.8 us
    pallas_call x3, Pallas kernels: 25.8 us -> 19.3 us  [call(): pl.pallas_call(kernel, out_shape=jax.ShapeDtypeStruct(shape, jnp.float32)...]
    unnamed x12 -> x0, local copies, waits for them, and re-layouts: 2.24 us -> none
    pallas_call x1, Pallas kernels: 4.35 us -> 2.91 us  [transposed(): pl.pallas_call(functools.partial(gram_kernel, nz, bands), out_shape=(jax....]
    all_to_all x1, blocking collectives: 16.1 us -> 14.8 us  [transposed(): lax.all_to_all(partial.reshape(holders, rows // holders, LANES), same_cor...]
  transfers between devices with their start and end apart: 4 -> 4, of which waited for: 3 -> 3; matrix products, arithmetic and copies ran while one was open for 1% -> 0% of each run, Pallas kernels for 0% -> 0%
where the time goes in v5:
time: 95.6 us; the launch traced here: 95.3 us
  blocking collectives  52.8 us (55%)
  Pallas kernels  23.8 us (25%)
  waiting for transfers between devices  13.3 us (14%)
  starting transfers between devices  5.35 us (6%)
    all_to_all x1, blocking collectives, transposed(): packed = lax.all_to_all(packed, area, 0, 0, tiled=True)  21.4 us
    pallas_call x3, Pallas kernels, call(): pl.pallas_call(kernel, out_shape=jax.ShapeDtypeStruct(shape, jnp.float32)...  19.3 us
    all_to_all x1, blocking collectives, transposed(): filtered = lax.all_to_all(filtered, everyone, 0, 0, tiled=True)  16.6 us
    all_to_all x1, blocking collectives, transposed(): lax.all_to_all(partial.reshape(holders, rows // holders, LANES), same_cor...  14.8 us
    all_to_all x1, waiting for transfers between devices, transposed(): mine = lax.all_to_all(pieces, same_core, 0, 0, tiled=True)  8.77 us
    all_to_all x1, starting transfers between devices, transposed(): mine = lax.all_to_all(pieces, same_core, 0, 0, tiled=True)  3.54 us
    pallas_call x1, Pallas kernels, transposed(): pl.pallas_call(functools.partial(gram_kernel, nz, bands), out_shape=(jax....  2.91 us
    ppermute x1, waiting for transfers between devices, transposed(): other = lax.ppermute(own, 'band', swap)  2.87 us
  transfers between devices with their start and end apart: 4, of which 3 were waited for; matrix products, arithmetic and copies ran while one was open for 0% of the time, Pallas kernels for 0%

profile of v5, /device:TPU:0, one launch (start us, length us, event | category | flops | bytes accessed | tf_op | source)
XLA Modules:
  0.0 95.3 jit_solution(8245533033417952791)
XLA Ops:
  0.0 1.6 %shard_map.28 = f32[16,56,128]{2,1,0:T(8,128)S(1)} custom-call(f32[384,256]{1,0:T(8,128)} %bitcast.6, f32[6,8,8]{2,1,0:T(8,128)} %potential_in.1), custom_call_target="tpu_custom_call" | custom-call | tf_op jit(solution)/shard_map/pallas_call | solution.py:391
  1.6 21.4 %all_to_all.20.in_ref = f32[16,56,128]{2,1,0:T(8,128)S(1)} all-to-all(f32[16,56,128]{2,1,0:T(8,128)S(1)} %shard_map.28), channel_id=1, replica_groups=mesh['chip'=2,'core'=2,'dy'=4,'band'=2] {'chip','core','dy'}, dimensions={0} | all-to-all | bytes 917504 | tf_op jit(solution)/shard_map/all_to_all | solution.py:403
  22.9 3.5 %shard_map.29 = f32[32,24,128]{2,1,0:T(8,128)S(1)} custom-call(f32[16,56,128]{2,1,0:T(8,128)S(1)} %all_to_all.20.in_ref), custom_call_target="tpu_custom_call" | custom-call | tf_op jit(solution)/shard_map/pallas_call | solution.py:367
  26.4 16.6 %all_to_all.21.own_ref = f32[32,24,128]{2,1,0:T(8,128)S(1)} all-to-all(f32[32,24,128]{2,1,0:T(8,128)S(1)} %shard_map.29), channel_id=1, replica_groups=mesh['chip'=2,'core'=2,'dy'=4,'band'=2] {'chip','core','dy','band'}, dimensions={0} | all-to-all | bytes 786432 | tf_op jit(solution)/shard_map/all_to_all | solution.py:414
  43.0 0.0 collective-permute-start
  43.0 0.1 pad_add_fusion.core_ref.place_ref
  43.1 1.6 %collective-permute-done.other_ref = f32[32,24,128]{2,1,0:T(8,128)S(1)} collective-permute-done((f32[32,24,128]{2,1,0:T(8,128)S(1)}, f32[32,24,128]{2,1,0:T(8,128)S(1)}, u32[]{:S(2)}, u32[]{:S(2)}) %collective-permute-start) | collective-permute-done | bytes 393248 | tf_op jit(solution)/shard_map/ppermute | solution.py:419
  44.8 2.9 %shard_map.30 = (f32[4,192,128]{2,1,0:T(8,128)S(1)}, f32[640,128]{1,0:T(8,128)S(1)}) custom-call(s32[2]{0:T(128)S(1)} %pad_add_fusion.core_ref.place_ref, f32[32,24,128]{2,1,0:T(8,128)S(1)} %all_to_all.21.own_ref, f32[32,24,128]{2,1,0:T(8,128)S(1)} %collective-permute-done.other_ref), custom_call_target="tpu_custom_call" | custom-call | tf_op jit(solution)/shard_map/pallas_call | solution.py:420
  47.7 14.8 %all_to_all.22.in_ref = f32[16,40,128]{2,1,0:T(8,128)S(1)} all-to-all(f32[16,40,128]{2,1,0:T(8,128)S(1)} %bitcast.5), channel_id=1, replica_groups=mesh['chip'=2,'core'=2,'dy'=4,'band'=2] {'chip','dy','band'}, dimensions={0} | all-to-all | bytes 655360 | tf_op jit(solution)/shard_map/all_to_all | solution.py:432
  62.5 0.8 shard_map.31
  63.2 3.5 %all-to-all-start.3 = ((f32[16,40,128]{2,1,0:T(8,128)}), f32[16,40,128]{2,1,0:T(8,128)S(1)}, u32[]{:S(2)}, u32[]{:S(2)}) async-start(f32[16,40,128]{2,1,0:T(8,128)} %shard_map.31), calls=%async_computation.3 | async-start | bytes 655360 | tf_op jit(solution)/shard_map/all_to_all | solution.py:434
  66.8 1.8 %collective-permute-start.2 = (f32[4,192,128]{2,1,0:T(8,128)S(1)}, f32[4,192,128]{2,1,0:T(8,128)S(1)}, u32[]{:S(2)}, u32[]{:S(2)}) collective-permute-start(f32[4,192,128]{2,1,0:T(8,128)S(1)} %get-tuple-element.8.own_ref), channel_id=1, source_target_pairs={{0,1},{1,0},{2,3},{3,2},{4,5},{5,4},{6,7},{7,6},{8,9},{9,8},{10,11... | collective-permute-start | bytes 1179656 | tf_op jit(solution)/shard_map/ppermute | solution.py:431
  68.6 8.8 %all-to-all-done.3.mine_ref = f32[16,40,128]{2,1,0:T(8,128)S(1)} async-done(((f32[16,40,128]{2,1,0:T(8,128)}), f32[16,40,128]{2,1,0:T(8,128)S(1)}, u32[]{:S(2)}, u32[]{:S(2)}) %all-to-all-start.3) | async-done | bytes 327712 | tf_op jit(solution)/shard_map/all_to_all | solution.py:434
  77.4 0.0 collective-permute-start.1
  77.4 2.9 %collective-permute-done.2.other_ref = f32[4,192,128]{2,1,0:T(8,128)S(1)} collective-permute-done((f32[4,192,128]{2,1,0:T(8,128)S(1)}, f32[4,192,128]{2,1,0:T(8,128)S(1)}, u32[]{:S(2)}, u32[]{:S(2)}) %collective-permute-start.2) | collective-permute-done | bytes 393248 | tf_op jit(solution)/shard_map/ppermute | solution.py:431
  80.2 0.0 collective-permute-done.1.theirs_ref
  80.2 15.1 %shard_map.32 = f32[384,256]{1,0:T(8,128)} custom-call(s32[2]{0:T(128)S(1)} %pad_add_fusion.core_ref.place_ref, f32[16,40,128]{2,1,0:T(8,128)S(1)} %all-to-all-done.3.mine_ref, f32[16,40,128]{2,1,0:T(8,128)S(1)} %collective-permute-done.1.theirs_ref, f32[4,192,128]{2,1,0:T(8,128)S(1)} %get-tuple-element.8.own_ref, ...), custom_call_target="tpu_custom_call" | custom-call | tf_op jit(solution)/shard_map/pallas_call | solution.py:367
Async XLA Ops:
  43.0 1.7 %collective-permute-start = (f32[32,24,128]{2,1,0:T(8,128)S(1)}, f32[32,24,128]{2,1,0:T(8,128)S(1)}, u32[]{:S(2)}, u32[]{:S(2)}) collective-permute-start(f32[32,24,128]{2,1,0:T(8,128)S(1)} %all_to_all.21.own_ref), channel_id=1, source_target_pairs={{0,8},{8,0},{1,9},{9,1},{2,10},{10,2},{3,11},{11,3},{4,12},{12,4},... | collective-permute-start | bytes 1179656 | tf_op jit(solution)/shard_map/ppermute | solution.py:419
  63.2 14.1 %all-to-all-start.3 = ((f32[16,40,128]{2,1,0:T(8,128)}), f32[16,40,128]{2,1,0:T(8,128)S(1)}, u32[]{:S(2)}, u32[]{:S(2)}) async-start(f32[16,40,128]{2,1,0:T(8,128)} %shard_map.31), calls=%async_computation.3 | async-start | bytes 655360 | tf_op jit(solution)/shard_map/all_to_all | solution.py:434
  66.8 13.4 %collective-permute-start.2 = (f32[4,192,128]{2,1,0:T(8,128)S(1)}, f32[4,192,128]{2,1,0:T(8,128)S(1)}, u32[]{:S(2)}, u32[]{:S(2)}) collective-permute-start(f32[4,192,128]{2,1,0:T(8,128)S(1)} %get-tuple-element.8.own_ref), channel_id=1, source_target_pairs={{0,1},{1,0},{2,3},{3,2},{4,5},{5,4},{6,7},{7,6},{8,9},{9,8},{10,11... | collective-permute-start | bytes 1179656 | tf_op jit(solution)/shard_map/ppermute | solution.py:431
  77.4 2.9 %collective-permute-start.1 = (f32[16,40,128]{2,1,0:T(8,128)S(1)}, f32[16,40,128]{2,1,0:T(8,128)S(1)}, u32[]{:S(2)}, u32[]{:S(2)}) collective-permute-start(f32[16,40,128]{2,1,0:T(8,128)S(1)} %all-to-all-done.3.mine_ref), channel_id=1, source_target_pairs={{0,8},{8,0},{1,9},{9,1},{2,10},{10,2},{3,11},{11,3},{4,12},{12,4},... | collective-permute-start | bytes 983048 | tf_op jit(solution)/shard_map/ppermute | solution.py:435

commit v6 on v5

--- a/solution.py
+++ b/solution.py
@@ -194,16 +194,17 @@
                 out_ref[i * shares + x % size_x // share, row : row + size_y, :] = result[size_y * j : size_y * (j + 1)]
 
 
-def unpack(nz, in_ref, bands, strip, out_ref, offset):
-    per_band = nz_strips(in_ref, nz, bands)
+def unpack(nz, bands, in_ref, strip):
+    per_band = in_ref.shape[0] // (nz * bands)
     first = nz * (strip % per_band)
     arrays = [in_ref[(first + g) * bands + strip // per_band] for g in range(nz)]
-    for z, value in enumerate(swap_groups(arrays, LANES // nz)):
-        out_ref[strip, pl.ds(offset + z, in_ref.shape[1], stride=nz), :] = value
-
-
-def nz_strips(in_ref, nz, bands):
-    return in_ref.shape[0] // (nz * bands)
+    return swap_groups(arrays, LANES // nz)
+
+
+def unpack_kernel(nz, bands, in_ref, out_ref):
+    for strip in range(out_ref.shape[0]):
+        for z, value in enumerate(unpack(nz, bands, in_ref, strip)):
+            out_ref[strip, pl.ds(z, in_ref.shape[1], stride=nz), :] = value
 
 
 def upper_blocks(strips):
@@ -214,13 +215,10 @@
     return upper_blocks(strips)[core :: CORES]
 
 
-def gram_kernel(nz, bands, core_ref, own_ref, other_ref, cells_ref, out_ref, paired):
-    strips, rows, _ = cells_ref.shape
-    for strip in range(strips):
-        unpack(nz, own_ref, bands, strip, paired, 0)
-        unpack(nz, other_ref, bands, strip, paired, rows)
-        cells_ref[strip] = paired[strip, :rows, :]
-    parts = [split(paired[strip]) for strip in range(strips)]
+def gram_kernel(nz, bands, core_ref, own_ref, other_in, out_ref, other_ref):
+    strips = own_ref.shape[0]
+    unpack_kernel(nz, bands, other_in, other_ref)
+    parts = [split(jnp.concatenate([own_ref[strip], other_ref[strip]], axis=0)) for strip in range(strips)]
     for core in range(CORES):
 
         @pl.when(core_ref[0] == core)
@@ -328,9 +326,19 @@
                 matrix[target, first:] = matrix[target, first:] - update
 
 
-def finish_kernel(place_ref, mine_ref, theirs_ref, own_ref, other_ref, out_ref, matrix, inverse):
-    strips = own_ref.shape[0]
-    cells = own_ref.shape[1]
+def prepare_kernel(place_ref, own_ref, first_ref, second_ref, *out_refs):
+    strips, cells, _ = own_ref.shape
+    band = place_ref[1]
+    for strip in range(strips):
+        received = first_ref if strip < strips // 2 else second_ref
+        for share, value in ((band, own_ref[strip]), (1 - band, received[strip % (strips // 2)])):
+            rows = pl.ds(pl.multiple_of(share * cells, cells), cells)
+            for ref, part in zip(out_refs, split(value)):
+                ref[strip, rows, :] = part
+
+
+def finish_kernel(place_ref, mine_ref, theirs_ref, high_ref, middle_ref, low_ref, out_ref, matrix, inverse):
+    strips = high_ref.shape[0]
     block = out_ref.shape[1]
     rows = mine_ref.shape[1]
     for core in range(CORES):
@@ -351,10 +359,19 @@
         @pl.when(band == b)
         def _(b=b):
             used = block * (b + 1)
-            mine = inverse[block * b : used, :used]
-            for share, ref in ((b, own_ref), (1 - b, other_ref)):
-                value = jnp.concatenate([ref[s] for s in range(used // LANES)], axis=1)
-                out_ref[cells * share : cells * (share + 1), :] = dot(value, mine, ((1,), (1,)))
+            left = left_parts(
+                [
+                    jnp.concatenate([ref[s] for s in range(used // LANES)], axis=1)
+                    for ref in (high_ref, middle_ref, low_ref)
+                ]
+            )
+            right = right_parts(split(inverse[block * b : used, :used]))
+            out_ref[...] = lax.dot_general(
+                jnp.concatenate(left, axis=1),
+                jnp.concatenate(right, axis=1),
+                (((1,), (1,)), ((), ())),
+                preferred_element_type=jnp.float32,
+            )
 
 
 def factor_kernel(in_ref, out_ref, matrix):
@@ -417,30 +434,39 @@
     rows = len(share_of(strips, 0)) * LANES
     holders = domains * bands // CORES
     neighbours = lax.ppermute(filtered, "core", swap)
-    own, partial = pl.pallas_call(
+    split_cells = (strips, cells // bands, LANES)
+    own = call(functools.partial(unpack_kernel, nz, bands), split_cells, filtered)
+    partial = call(
         functools.partial(gram_kernel, nz, bands),
-        out_shape=(
-            jax.ShapeDtypeStruct((strips, cells // bands, LANES), jnp.float32),
-            jax.ShapeDtypeStruct((rows, LANES), jnp.float32),
-        ),
-        in_specs=[SMEM, VMEM, VMEM],
-        out_specs=(VMEM, VMEM),
-        scratch_shapes=[pltpu.VMEM((strips, CORES * cells // bands, LANES), jnp.float32)],
-        compiler_params=ROOM,
-    )(place, filtered, neighbours)
-    other = lax.ppermute(own, "band", swap)
+        (rows, LANES),
+        place,
+        own,
+        neighbours,
+        scratch=[pltpu.VMEM(split_cells, jnp.float32)],
+        scalars=1,
+    )
+    first, second = jnp.split(own, 2)
+    first = lax.ppermute(first, "band", swap)
+    second = lax.ppermute(second, "band", swap)
     partial = lax.all_to_all(partial.reshape(holders, rows // holders, LANES), same_core, 0, 0, tiled=True)
     pieces = call(functools.partial(sum_kernel, float(cells * domains)), partial.shape, partial)
     mine = lax.all_to_all(pieces, same_core, 0, 0, tiled=True)
     theirs = lax.ppermute(mine, "core", swap)
+    whole_cells = (strips, cells, LANES)
+    parts = pl.pallas_call(
+        prepare_kernel,
+        out_shape=[jax.ShapeDtypeStruct(whole_cells, jnp.bfloat16)] * 3,
+        in_specs=[SMEM] + [VMEM] * 3,
+        out_specs=[VMEM] * 3,
+        compiler_params=ROOM,
+    )(place, own, first, second)
     result = call(
         finish_kernel,
         (cells, block),
         place,
         mine,
         theirs,
-        own,
-        other,
+        *parts,
         scratch=[pltpu.VMEM((size, size), jnp.float32)] * 2,
         scalars=1,
     )
@@ -514,6 +540,7 @@
             and block % LANES == 0
             and bands == 2
             and size_x % bands == 0
+            and size // LANES % 2 == 0
             and domains_x % CORES == 0
             and (size // LANES) * (size // LANES + 1) * LANES % (2 * domains * bands * SUBLANES) == 0
             and total_x > 2 * WIDTH

time: 95.6 us -> 103 us (1.077)
  blocking collectives: 52.8 us -> 66.7 us
  starting transfers between devices: 5.35 us -> 2.1 us
  waiting for transfers between devices: 13.3 us -> 10.5 us
    all_to_all x0 -> x1, blocking collectives: none -> 13.9 us  [transposed(): mine = lax.all_to_all(pieces, same_core, 0, 0, tiled=True)]
    all_to_all x1 -> x0, waiting for transfers between devices: 8.77 us -> none  [transposed(): mine = lax.all_to_all(pieces, same_core, 0, 0, tiled=True)]
    ppermute x1 -> x2, waiting for transfers between devices: 2.87 us -> 9.5 us  [the longest x1 5.75 us: transposed(): first = lax.ppermute(first, 'band', swap)]
    all_to_all x1 -> x0, starting transfers between devices: 3.54 us -> none  [transposed(): mine = lax.all_to_all(pieces, same_core, 0, 0, tiled=True)]
    pallas_call x1, Pallas kernels: 2.91 us -> 0.68 us  [transposed(): pl.pallas_call(prepare_kernel, out_shape=[jax.ShapeDtypeStruct(whole_cell...]
    pallas_call x3 -> x5, Pallas kernels: 19.3 us -> 21.2 us  [call(): pl.pallas_call(kernel, out_shape=jax.ShapeDtypeStruct(shape, jnp.float32)...]
    ppermute x1 -> x2, starting transfers between devices: 1.81 us -> 2.09 us  [the longest x1 1.46 us: transposed(): second = lax.ppermute(second, 'band', swap)]
  transfers between devices with their start and end apart: 4 -> 4, of which waited for: 3 -> 3; matrix products, arithmetic and copies ran while one was open for 0% -> 0% of each run, Pallas kernels for 0% -> 1%
where the time goes in v6:
time: 103 us
  blocking collectives  66.7 us (65%)
  Pallas kernels  23.5 us (23%)
  waiting for transfers between devices  10.5 us (10%)
  starting transfers between devices  2.1 us (2%)
    all_to_all x1, blocking collectives, transposed(): packed = lax.all_to_all(packed, area, 0, 0, tiled=True)  21.4 us
    pallas_call x5, Pallas kernels, call(): pl.pallas_call(kernel, out_shape=jax.ShapeDtypeStruct(shape, jnp.float32)...  21.2 us
    all_to_all x1, blocking collectives, transposed(): filtered = lax.all_to_all(filtered, everyone, 0, 0, tiled=True)  16.6 us
    all_to_all x1, blocking collectives, transposed(): lax.all_to_all(partial.reshape(holders, rows // holders, LANES), same_cor...  14.8 us
    all_to_all x1, blocking collectives, transposed(): mine = lax.all_to_all(pieces, same_core, 0, 0, tiled=True)  13.9 us
    ppermute x1, waiting for transfers between devices, transposed(): first = lax.ppermute(first, 'band', swap)  5.75 us
    ppermute x1, waiting for transfers between devices, transposed(): second = lax.ppermute(second, 'band', swap)  3.75 us
  transfers between devices with their start and end apart: 4, of which 3 were waited for; matrix products, arithmetic and copies ran while one was open for 0% of the time, Pallas kernels for 1%

profile of v6, /device:TPU:0, one launch (start us, length us, event | category | flops | bytes accessed | tf_op | source)
XLA Modules:
  0.0 102.9 jit_solution(15037767315868934490)
XLA Ops:
  0.0 1.6 %shard_map.28 = f32[16,56,128]{2,1,0:T(8,128)S(1)} custom-call(f32[384,256]{1,0:T(8,128)} %bitcast.6, f32[6,8,8]{2,1,0:T(8,128)} %potential_in.1), custom_call_target="tpu_custom_call" | custom-call | tf_op jit(solution)/shard_map/pallas_call | solution.py:408
  1.6 21.4 %all_to_all.20.in_ref = f32[16,56,128]{2,1,0:T(8,128)S(1)} all-to-all(f32[16,56,128]{2,1,0:T(8,128)S(1)} %shard_map.28), channel_id=1, replica_groups=mesh['chip'=2,'core'=2,'dy'=4,'band'=2] {'chip','core','dy'}, dimensions={0} | all-to-all | bytes 917504 | tf_op jit(solution)/shard_map/all_to_all | solution.py:420
  22.9 3.5 %shard_map.29 = f32[32,24,128]{2,1,0:T(8,128)S(1)} custom-call(f32[16,56,128]{2,1,0:T(8,128)S(1)} %all_to_all.20.in_ref), custom_call_target="tpu_custom_call" | custom-call | tf_op jit(solution)/shard_map/pallas_call | solution.py:384
  26.4 16.6 %all_to_all.21.in_ref = f32[32,24,128]{2,1,0:T(8,128)S(1)} all-to-all(f32[32,24,128]{2,1,0:T(8,128)S(1)} %shard_map.29), channel_id=1, replica_groups=mesh['chip'=2,'core'=2,'dy'=4,'band'=2] {'chip','core','dy','band'}, dimensions={0} | all-to-all | bytes 786432 | tf_op jit(solution)/shard_map/all_to_all | solution.py:431
  43.0 0.0 collective-permute-start
  43.0 0.1 pad_add_fusion.core_ref.place_ref
  43.1 0.6 shard_map.30.own_ref
  43.7 1.0 %collective-permute-done.other_in = f32[32,24,128]{2,1,0:T(8,128)S(1)} collective-permute-done((f32[32,24,128]{2,1,0:T(8,128)S(1)}, f32[32,24,128]{2,1,0:T(8,128)S(1)}, u32[]{:S(2)}, u32[]{:S(2)}) %collective-permute-start) | collective-permute-done | bytes 393248 | tf_op jit(solution)/shard_map/ppermute | solution.py:436
  44.8 2.2 %shard_map.31 = f32[640,128]{1,0:T(8,128)S(1)} custom-call(s32[2]{0:T(128)S(1)} %pad_add_fusion.core_ref.place_ref, f32[4,192,128]{2,1,0:T(8,128)S(1)} %shard_map.30.own_ref, f32[32,24,128]{2,1,0:T(8,128)S(1)} %collective-permute-done.other_in), custom_call_target="tpu_custom_call" | custom-call | tf_op jit(solution)/shard_map/pallas_call | solution.py:384
  47.0 14.8 %all_to_all.22.in_ref = f32[16,40,128]{2,1,0:T(8,128)S(1)} all-to-all(f32[16,40,128]{2,1,0:T(8,128)S(1)} %bitcast.5), channel_id=1, replica_groups=mesh['chip'=2,'core'=2,'dy'=4,'band'=2] {'chip','dy','band'}, dimensions={0} | all-to-all | bytes 655360 | tf_op jit(solution)/shard_map/all_to_all | solution.py:451
  61.8 13.9 %all_to_all.23.mine_ref = f32[16,40,128]{2,1,0:T(8,128)S(1)} all-to-all(f32[16,40,128]{2,1,0:T(8,128)S(1)} %shard_map.32), channel_id=1, replica_groups=mesh['chip'=2,'core'=2,'dy'=4,'band'=2] {'chip','dy','band'}, dimensions={0} | all-to-all | bytes 655360 | tf_op jit(solution)/shard_map/all_to_all | solution.py:453
  75.7 0.0 collective-permute-start.1
  75.7 0.6 collective-permute-start.2
  76.4 1.5 %collective-permute-start.3 = (f32[2,192,128]{2,1,0:T(8,128)S(1)}, f32[2,192,128]{2,1,0:T(8,128)S(1)}, u32[]{:S(2)}, u32[]{:S(2)}) collective-permute-start(f32[2,192,128]{2,1,0:T(8,128)S(1)} %get-tuple-element.11), channel_id=1, source_target_pairs={{0,1},{1,0},{2,3},{3,2},{4,5},{5,4},{6,7},{7,6},{8,9},{9,8},{10,11... | collective-permute-start | bytes 589832 | tf_op jit(solution)/shard_map/ppermute | solution.py:450
  77.8 5.7 %collective-permute-done.2.first_ref = f32[2,192,128]{2,1,0:T(8,128)S(1)} collective-permute-done((f32[2,192,128]{2,1,0:T(8,128)S(1)}, f32[2,192,128]{2,1,0:T(8,128)S(1)}, u32[]{:S(2)}, u32[]{:S(2)}) %collective-permute-start.2) | collective-permute-done | bytes 196640 | tf_op jit(solution)/shard_map/ppermute | solution.py:449
  83.6 3.8 %collective-permute-done.3.second_ref = f32[2,192,128]{2,1,0:T(8,128)S(1)} collective-permute-done((f32[2,192,128]{2,1,0:T(8,128)S(1)}, f32[2,192,128]{2,1,0:T(8,128)S(1)}, u32[]{:S(2)}, u32[]{:S(2)}) %collective-permute-start.3) | collective-permute-done | bytes 196640 | tf_op jit(solution)/shard_map/ppermute | solution.py:450
  87.3 0.7 shard_map.33
  88.0 0.0 collective-permute-done.1.theirs_ref
  88.0 14.9 %shard_map.34 = f32[384,256]{1,0:T(8,128)} custom-call(s32[2]{0:T(128)S(1)} %pad_add_fusion.core_ref.place_ref, f32[16,40,128]{2,1,0:T(8,128)S(1)} %all_to_all.23.mine_ref, f32[16,40,128]{2,1,0:T(8,128)S(1)} %collective-permute-done.1.theirs_ref, bf16[4,384,128]{2,1,0:T(8,128)(2,1)S(1)} %get-tuple-element.8.high_ref, ...), custom_call_target="tpu_custom_call" | custom-call | tf_op jit(solution)/shard_map/pallas_call | solution.py:384
  (2 shorter events, 0.1 us)
Async XLA Ops:
  43.0 1.7 %collective-permute-start = (f32[32,24,128]{2,1,0:T(8,128)S(1)}, f32[32,24,128]{2,1,0:T(8,128)S(1)}, u32[]{:S(2)}, u32[]{:S(2)}) collective-permute-start(f32[32,24,128]{2,1,0:T(8,128)S(1)} %all_to_all.21.in_ref), channel_id=1, source_target_pairs={{0,8},{8,0},{1,9},{9,1},{2,10},{10,2},{3,11},{11,3},{4,12},{12,4},... | collective-permute-start | bytes 1179656 | tf_op jit(solution)/shard_map/ppermute | solution.py:436
  75.7 12.3 %collective-permute-start.1 = (f32[16,40,128]{2,1,0:T(8,128)S(1)}, f32[16,40,128]{2,1,0:T(8,128)S(1)}, u32[]{:S(2)}, u32[]{:S(2)}) collective-permute-start(f32[16,40,128]{2,1,0:T(8,128)S(1)} %all_to_all.23.mine_ref), channel_id=1, source_target_pairs={{0,8},{8,0},{1,9},{9,1},{2,10},{10,2},{3,11},{11,3},{4,12},{12,4},... | collective-permute-start | bytes 983048 | tf_op jit(solution)/shard_map/ppermute | solution.py:454
  75.7 7.8 %collective-permute-start.2 = (f32[2,192,128]{2,1,0:T(8,128)S(1)}, f32[2,192,128]{2,1,0:T(8,128)S(1)}, u32[]{:S(2)}, u32[]{:S(2)}) collective-permute-start(f32[2,192,128]{2,1,0:T(8,128)S(1)} %get-tuple-element.12), channel_id=1, source_target_pairs={{0,1},{1,0},{2,3},{3,2},{4,5},{5,4},{6,7},{7,6},{8,9},{9,8},{10,11... | collective-permute-start | bytes 589832 | tf_op jit(solution)/shard_map/ppermute | solution.py:449
  76.4 11.0 %collective-permute-start.3 = (f32[2,192,128]{2,1,0:T(8,128)S(1)}, f32[2,192,128]{2,1,0:T(8,128)S(1)}, u32[]{:S(2)}, u32[]{:S(2)}) collective-permute-start(f32[2,192,128]{2,1,0:T(8,128)S(1)} %get-tuple-element.11), channel_id=1, source_target_pairs={{0,1},{1,0},{2,3},{3,2},{4,5},{5,4},{6,7},{7,6},{8,9},{9,8},{10,11... | collective-permute-start | bytes 589832 | tf_op jit(solution)/shard_map/ppermute | solution.py:450
